TPU v7x, 32 devices: a whole 2x2x4 slice. The times are simulated.
32 devices in a mesh: dp: 16 (over z, y, core), mp: 2 (over x).
Axes of the slice: x: 2, y: 2, z: 4, core: 2. Of those that a mesh axis runs over, the one named last changes fastest.
Arguments:
- frames: bfloat16 [512, 16, 1024], P(('dp', 'mp')), may hold values from -6 to 6
- offsets: int32 [512, 16], P(('dp', 'mp')), may hold values from 1 to 2
- gain_attn: float32 [16, 1024], replicated, may hold values from 0.25 to 1.75
- w_qkv: bfloat16 [16, 3, 1024, 1024], P(None, None, 'dp', 'mp'), may hold values from -0.1875 to 0.1875
- w_out: bfloat16 [16, 1024, 1024], P(None, 'mp', 'dp'), may hold values from -0.375 to 0.375
- gain_ffn: float32 [16, 1024], replicated, may hold values from 0.25 to 1.75
- w_gu: bfloat16 [16, 2, 1024, 4096], P(None, None, 'dp', 'mp'), may hold values from -0.1875 to 0.1875
- w_down: bfloat16 [16, 4096, 1024], P(None, 'mp', 'dp'), may hold values from -0.1875 to 0.1875
- cotangent: bfloat16 [512, 16, 1024], P(('dp', 'mp')), may hold values from -6 to 6
Outputs:
- result: bfloat16 [512, 16, 1024], P(('dp', 'mp'))
- grad_frames: bfloat16 [512, 16, 1024], P(('dp', 'mp'))
- grad_gain_attn: float32 [16, 1024], P(None, ('dp', 'mp'))
- grad_w_qkv: float32 [16, 3, 1024, 1024], P(None, None, 'dp', 'mp')
- grad_w_out: float32 [16, 1024, 1024], P(None, 'mp', 'dp')
- grad_gain_ffn: float32 [16, 1024], P(None, ('dp', 'mp'))
- grad_w_gu: float32 [16, 2, 1024, 4096], P(None, None, 'dp', 'mp')
- grad_w_down: float32 [16, 4096, 1024], P(None, 'mp', 'dp')
All inputs are finite; a program needn't handle non-finite values.
Results may differ from a plain program's by a relative error of at most 0.02.
Values may be sent and summed in bfloat16 or wider, within the bound.
No kernel may reach another device: no remote copies, remote signals or barrier semaphores. Data moves between devices by JAX's collectives and lax.ppermute only.
A program may use at most 640 MiB of HBM per device.

v0:
```python
import jax
import jax.numpy as jnp
from jax import lax
from jax.sharding import PartitionSpec as P

HD = 64


norm_eps = 1e-06


def from_behind(value, axis, steps):
    count = lax.axis_size(axis)
    initial, last = (max(0, -steps), min(count, count - steps))
    return lax.ppermute(value, axis, [(source, source + steps) for source in range(initial, last)])


def delayed(frames, offsets):
    prior = from_behind(frames[-2:], ("dp", "mp"), 1)
    joined = jnp.concatenate([prior, frames], axis=0).astype(jnp.float32)
    row_count = frames.shape[0]
    return jnp.where((offsets == 1)[:, :, None], joined[1 : row_count + 1], joined[0:row_count])


def normalize(residual, norm_gain):
    scaling = lax.rsqrt(jnp.mean(residual * residual, axis=-1, keepdims=True) + norm_eps)
    unit_rows = residual * scaling
    return (unit_rows, scaling, (unit_rows * norm_gain).astype(jnp.bfloat16))


def norm_back(grad_normed, unit_rows, scaling, norm_gain):
    weighted = grad_normed * norm_gain
    inner_mean = jnp.mean(weighted * unit_rows, axis=-1, keepdims=True)
    return (scaling * (weighted - unit_rows * inner_mean), jnp.sum(grad_normed * unit_rows, axis=0))


def head_scores(qkv_low, head_width):
    frame_count = qkv_low.shape[0]
    positions = qkv_low.shape[1]
    head_count = qkv_low.shape[3] // head_width
    queries = qkv_low[:, :, 0].reshape(frame_count, positions, head_count, head_width)
    key_rows = qkv_low[:, :, 1].reshape(frame_count, positions, head_count, head_width)
    value_rows = qkv_low[:, :, 2].reshape(frame_count, positions, head_count, head_width)
    scaling = head_width ** (-0.5)
    scores = (
        jnp.einsum("fphe,fqhe->fhpq", queries, key_rows, preferred_element_type=jnp.float32)
        * scaling
    )
    causal = jnp.arange(positions)[:, None] >= jnp.arange(positions)[None, :]
    scores = jnp.where(causal, scores, -1e30)
    return (queries, key_rows, value_rows, scores, scaling)


def attend(qkv_low, head_width):
    queries, key_rows, value_rows, scores, scaling = head_scores(qkv_low, head_width)
    row_max = jnp.max(scores, axis=-1, keepdims=True)
    log_total = row_max + jnp.log(jnp.sum(jnp.exp(scores - row_max), axis=-1, keepdims=True))
    probs_low = jnp.exp(scores - log_total).astype(jnp.bfloat16)
    mixed = jnp.einsum("fhpq,fqhe->fphe", probs_low, value_rows, preferred_element_type=jnp.float32)
    mixed_low = mixed.reshape(qkv_low.shape[0], qkv_low.shape[1], qkv_low.shape[3]).astype(
        jnp.bfloat16
    )
    return (mixed_low, log_total)


def attend_back(qkv_low, grad_mixed, log_total, head_width):
    queries, key_rows, value_rows, scores, scaling = head_scores(qkv_low, head_width)
    attn_probs = jnp.exp(scores - log_total)
    probs_low = attn_probs.astype(jnp.bfloat16)
    grad_heads = grad_mixed.reshape(queries.shape)
    grad_values = jnp.einsum(
        "fhpq,fphe->fqhe", probs_low, grad_heads, preferred_element_type=jnp.float32
    )
    grad_probs = jnp.einsum(
        "fphe,fqhe->fhpq", grad_heads, value_rows, preferred_element_type=jnp.float32
    )
    row_inner = jnp.sum(attn_probs * grad_probs, axis=-1, keepdims=True)
    grad_scores = (attn_probs * (grad_probs - row_inner)).astype(jnp.bfloat16)
    grad_queries = (
        jnp.einsum("fhpq,fqhe->fphe", grad_scores, key_rows, preferred_element_type=jnp.float32)
        * scaling
    )
    grad_keys = (
        jnp.einsum("fhpq,fphe->fqhe", grad_scores, queries, preferred_element_type=jnp.float32)
        * scaling
    )
    stacked = jnp.stack([grad_queries, grad_keys, grad_values], axis=2)
    return stacked.reshape(qkv_low.shape).astype(jnp.bfloat16)


def body(frames, offsets, gain_attn, w_qkv, w_out, gain_ffn, w_gu, w_down, cotangent):
    row_count = frames.shape[0]
    resid_in = delayed(frames, offsets)
    unit_one, scale_one, normed_one = normalize(resid_in, gain_attn)
    group_norm, group_cot = (
        lax.all_gather(normed_one, "mp", axis=0, tiled=True),
        lax.all_gather(cotangent, "mp", axis=0, tiled=True),
    )
    full_qkv, full_out, full_gu, full_down = (
        lax.all_gather(w_qkv, "dp", axis=2, tiled=True),
        lax.all_gather(w_out, "dp", axis=2, tiled=True),
        lax.all_gather(w_gu, "dp", axis=2, tiled=True),
        lax.all_gather(w_down, "dp", axis=2, tiled=True),
    )
    qkv_low = jnp.einsum(
        "fpd,pjde->fpje", group_norm, full_qkv, preferred_element_type=jnp.float32
    ).astype(jnp.bfloat16)
    mixed_low, log_total = attend(qkv_low, HD)
    segment = mixed_low
    attn_sum = lax.psum_scatter(
        jnp.einsum("fpe,ped->fpd", segment, full_out, preferred_element_type=jnp.float32),
        "mp",
        scatter_dimension=0,
        tiled=True,
    )
    hidden_in = resid_in + attn_sum
    unit_two, scale_two, normed_two = normalize(hidden_in, gain_ffn)
    group_two = lax.all_gather(normed_two, "mp", axis=0, tiled=True)
    gate_up = jnp.einsum("fpd,pjde->fpje", group_two, full_gu, preferred_element_type=jnp.float32)
    gate_pre = gate_up[:, :, 0]
    up_pre = gate_up[:, :, 1]
    sigmoid_gate = jax.nn.sigmoid(gate_pre)
    silu_gate = gate_pre * sigmoid_gate
    hidden_low = (silu_gate * up_pre).astype(jnp.bfloat16)
    segment = hidden_low
    ffn_sum = lax.psum_scatter(
        jnp.einsum("fpe,ped->fpd", segment, full_down, preferred_element_type=jnp.float32).astype(
            jnp.bfloat16
        ),
        "mp",
        scatter_dimension=0,
        tiled=True,
    ).astype(jnp.float32)
    result = (hidden_in + ffn_sum).astype(jnp.bfloat16)
    grad_down = jnp.einsum(
        "fpe,fpd->ped", hidden_low, group_cot, preferred_element_type=jnp.float32
    )
    grad_hidden = jnp.einsum(
        "fpd,ped->fpe", group_cot, full_down, preferred_element_type=jnp.float32
    )
    slope = sigmoid_gate * (1.0 + gate_pre * (1.0 - sigmoid_gate))
    grad_gu = jnp.stack([grad_hidden * up_pre * slope, grad_hidden * silu_gate], axis=2).astype(
        jnp.bfloat16
    )
    grad_wgu = jnp.einsum("fpd,fpje->pjde", group_two, grad_gu, preferred_element_type=jnp.float32)
    ffn_grads = (grad_wgu, grad_down)
    segment = grad_gu
    grad_normed_two = lax.psum_scatter(
        jnp.einsum("fpje,pjde->fpd", segment, full_gu, preferred_element_type=jnp.float32).astype(
            jnp.bfloat16
        ),
        "mp",
        scatter_dimension=0,
        tiled=True,
    ).astype(jnp.float32)
    back_two, gain_two = norm_back(grad_normed_two, unit_two, scale_two, gain_ffn)
    grad_hidden_in = cotangent.astype(jnp.float32) + back_two
    group_grad = lax.all_gather(grad_hidden_in.astype(jnp.bfloat16), "mp", axis=0, tiled=True)
    grad_wout = jnp.einsum(
        "fpe,fpd->ped", mixed_low, group_grad, preferred_element_type=jnp.float32
    )
    grad_mixed = jnp.einsum(
        "fpd,ped->fpe", group_grad, full_out, preferred_element_type=jnp.float32
    ).astype(jnp.bfloat16)
    grad_qkv = attend_back(qkv_low, grad_mixed, log_total, HD)
    grad_wqkv = jnp.einsum(
        "fpd,fpje->pjde", group_norm, grad_qkv, preferred_element_type=jnp.float32
    )
    segment = grad_qkv
    grad_normed_one = lax.psum_scatter(
        jnp.einsum("fpje,pjde->fpd", segment, full_qkv, preferred_element_type=jnp.float32).astype(
            jnp.bfloat16
        ),
        "mp",
        scatter_dimension=0,
        tiled=True,
    ).astype(jnp.float32)
    back_one, gain_one = norm_back(grad_normed_one, unit_one, scale_one, gain_attn)
    grad_resid = grad_hidden_in + back_one
    one_step = jnp.where((offsets == 1)[:, :, None], grad_resid, 0.0)
    two_step = jnp.where((offsets == 2)[:, :, None], grad_resid, 0.0)
    spread = jnp.pad(one_step, ((1, 1), (0, 0), (0, 0))) + jnp.pad(
        two_step, ((0, 2), (0, 0), (0, 0))
    )
    returned = from_behind(spread[:2].astype(jnp.bfloat16), ("dp", "mp"), -1).astype(jnp.float32)
    grad_frames = (spread[2:] + jnp.pad(returned, ((row_count - 2, 0), (0, 0), (0, 0)))).astype(
        jnp.bfloat16
    )
    gain_sums = (
        lax.psum_scatter(gain_one, ("dp", "mp"), scatter_dimension=1, tiled=True),
        lax.psum_scatter(gain_two, ("dp", "mp"), scatter_dimension=1, tiled=True),
    )
    weight_sums = (
        lax.psum_scatter(
            grad_wqkv.astype(jnp.bfloat16), "dp", scatter_dimension=2, tiled=True
        ).astype(jnp.float32),
        lax.psum_scatter(
            grad_wout.astype(jnp.bfloat16), "dp", scatter_dimension=2, tiled=True
        ).astype(jnp.float32),
        lax.psum_scatter(
            ffn_grads[0].astype(jnp.bfloat16), "dp", scatter_dimension=2, tiled=True
        ).astype(jnp.float32),
        lax.psum_scatter(
            ffn_grads[1].astype(jnp.bfloat16), "dp", scatter_dimension=2, tiled=True
        ).astype(jnp.float32),
    )
    return (
        result,
        grad_frames,
        gain_sums[0],
        weight_sums[0],
        weight_sums[1],
        gain_sums[1],
        weight_sums[2],
        weight_sums[3],
    )


def solution(mesh):
    return jax.shard_map(
        body,
        mesh=mesh,
        in_specs=(
            P(("dp", "mp"), None, None),
            P(("dp", "mp"), None),
            P(),
            P(None, None, "dp", "mp"),
            P(None, "mp", "dp"),
            P(),
            P(None, None, "dp", "mp"),
            P(None, "mp", "dp"),
            P(("dp", "mp"), None, None),
        ),
        out_specs=(
            P(("dp", "mp"), None, None),
            P(("dp", "mp"), None, None),
            P(None, ("dp", "mp")),
            P(None, None, "dp", "mp"),
            P(None, "mp", "dp"),
            P(None, ("dp", "mp")),
            P(None, None, "dp", "mp"),
            P(None, "mp", "dp"),
        ),
        check_vma=False,
    )
```

profile of v0, /device:TPU:15, one launch (start us, length us, event | category | flops | bytes accessed | tf_op | source)
XLA Modules:
  0.0 4521.2 jit_solution(14130845077408396319)
XLA Ops:
  7.2 1.3 copy.73
  8.6 3.7 collective-permute-start
  12.3 1.3 broadcast_compare_fusion
  15.0 1.0 multiply_convert_fusion.5
  17.5 21.0 all-gather.9.cloned.1.call-done
  38.5 249.6 %all-gather.11.cloned.1.call-done = bf16[16,3,1024,512]{3,2,1,0:T(8,128)(2,1)} async-done(((bf16[16,3,64,512]{3,2,1,0:T(8,128)(2,1)}), bf16[16,3,1024,512]{3,2,1,0:T(8,128)(2,1)}) %all-gather.11.cloned.1.call-update) | async-done | bytes 50331664 | tf_op jit(solution)/shard_map/all_gather | solution.py:100
  288.1 20.8 fusion.12
  308.9 1.1 fusion.56
  310.0 2.4 reshape_squeeze.13
  312.4 2.4 reshape_squeeze.14
  314.8 1.5 reshape_squeeze.12
  316.3 3.2 fusion.57
  321.7 1.3 copy.118
  323.0 2.6 reshape.83
  325.5 89.2 %all-gather.13.cloned.1.call-done = bf16[16,512,1024]{1,2,0:T(8,128)(2,1)} async-done(((bf16[16,512,64]{1,2,0:T(8,128)(2,1)}), bf16[16,512,1024]{1,2,0:T(8,128)(2,1)}) %all-gather.13.cloned.1.call-update) | async-done | bytes 16777232 | tf_op jit(solution)/shard_map/all_gather | solution.py:101
  414.7 12.2 convolution_bitcast_fusion.1
  427.3 31.1 reduce-scatter.19.cloned.1.call-done
  458.3 1.4 multiply_reduce_fusion.1
  459.8 1.0 copy-done.3
  462.8 1.1 copy.82
  464.7 18.5 all-gather.15.cloned.1.call-done
  483.2 644.2 %all-gather.17.cloned.1.call-done = bf16[16,2,1024,2048]{3,2,1,0:T(8,128)(2,1)} async-done(((bf16[16,2,64,2048]{3,2,1,0:T(8,128)(2,1)}), bf16[16,2,1024,2048]{3,2,1,0:T(8,128)(2,1)}) %all-gather.17.cloned.1.call-update) | async-done | bytes 134217744 | tf_op jit(solution)/shard_map/all_gather | solution.py:102
  1127.4 49.3 %convolution_bitcast_fusion = f32[32,16,2,2048]{3,0,2,1:T(8,128)} fusion(bf16[16,2,1024,2048]{3,2,1,0:T(8,128)(2,1)} %all-gather.17.cloned.1.call-done, bf16[32,16,1024]{2,0,1:T(8,128)(2,1)} %all-gather.15.cloned.1.call-done), kind=kOutput, calls=%fused_computation.6 | convolution fusion | flops 4294967296 | bytes 143654912 | tf_op jit(solution)/shard_map/fpd,pjde->fpje/dot_general | solution.py:119
  1176.8 301.9 %all-gather.19.cloned.1.call-done = bf16[16,2048,1024]{1,2,0:T(8,128)(2,1)} async-done(((bf16[16,2048,64]{1,2,0:T(8,128)(2,1)}), bf16[16,2048,1024]{1,2,0:T(8,128)(2,1)}) %all-gather.19.cloned.1.call-update) | async-done | bytes 67108880 | tf_op jit(solution)/shard_map/all_gather | solution.py:103
  1478.7 28.7 fusion.8
  1507.4 56.0 %fusion.19 = bf16[32,16,1024]{2,0,1:T(8,128)(2,1)} fusion(bf16[16,2,1024,2048]{3,2,1,0:T(8,128)(2,1)} %all-gather.17.cloned.1.call-done, bf16[32,16,1,2048]{3,0,1,2:T(8,128)(2,1)} %get-tuple-element.43, bf16[32,16,1,2048]{3,0,1,2:T(8,128)(2,1)} %get-tuple-element.42), kind=kOutput, calls=%fused_computation.45 | convolution fusion | flops 4297588736 | bytes 139460608 | tf_op jit(solution)/shard_map/fpje,pjde->fpd/dot_general | solution.py:149
  1563.5 19.7 reduce-scatter.23.cloned.1.call-done
  1583.2 1.6 fusion.33
  1585.5 1.3 fusion.54
  1587.3 21.0 all-gather.23.cloned.1.call-done
  1608.2 9.7 fusion.26
  1617.9 1.6 reshape.69
  1620.8 1.7 multiply_reduce_fusion
  1626.2 1.4 reshape.76
  1627.8 1.4 reshape.74
  1632.8 22.1 fusion.13
  1655.1 28.4 fusion.18
  1683.6 1.0 copy.116
  1684.8 2.1 fusion.34
  1686.9 1.0 copy.114
  1688.0 12.1 convolution_convert_fusion.1
  1700.2 1.1 copy-done.11
  1701.3 21.9 convert_bitcast_fusion.1
  1723.2 62.3 %copy.98 = bf16[16,3,1024,512]{3,0,1,2:T(8,128)(2,1)} copy(bf16[16,3,1024,512]{2,3,1,0:T(8,128)(2,1)} %convert_bitcast_fusion.1) | data formatting | bytes 100663296 | tf_op jit(solution)/shard_map/convert_element_type | solution.py:195
  1785.6 1.1 copy-done.10
  1786.7 25.1 convolution_convert_fusion
  1812.1 1.3 copy-done.9
  1813.7 53.1 %convert_bitcast_fusion = bf16[16,2,1024,2048]{2,3,1,0:T(8,128)(2,1)} fusion(bf16[32,16,1024]{2,0,1:T(8,128)(2,1)S(1)} %copy-done.15, bf16[32,16,1,2048]{3,0,1,2:T(8,128)(2,1)} %get-tuple-element.43, bf16[32,16,1,2048]{3,0,1,2:T(8,128)(2,1)S(1)} %copy-done.9), kind=kOutput, calls=%fused_computation.2 | convolution fusion | flops 4364173312 | bytes 139460608 | tf_op jit(solution)/shard_map/fpd,fpje->pjde/dot_general | solution.py:145
  1866.8 192.5 %copy.101 = bf16[16,2,1024,2048]{3,0,1,2:T(8,128)(2,1)} copy(bf16[16,2,1024,2048]{2,3,1,0:T(8,128)(2,1)} %convert_bitcast_fusion) | data formatting | bytes 268435456 | tf_op jit(solution)/shard_map/convert_element_type | solution.py:201
  2060.9 3.1 broadcast_select_fusion
  2064.2 3.0 collective-permute-start.1
  2067.3 1.4 copy.117
  2068.7 1.1 copy.102
  2069.7 4.8 collective-permute-done.1
  2074.9 1.1 copy.103
  2076.0 1.4 copy.115
  2077.4 77.2 %reduce-scatter.27.cloned.1.call-done = bf16[16,512,64]{1,2,0:T(8,128)(2,1)} async-done(((bf16[16,512,1024]{1,2,0:T(8,128)(2,1)}), bf16[16,512,64]{1,2,0:T(8,128)(2,1)}) %reduce-scatter.27.cloned.1.call-update) | async-done | bytes 1048592 | tf_op jit(solution)/shard_map/reduce_scatter | solution.py:197
  2154.5 2.8 convert_element_type.149
  2157.4 465.7 %reduce-scatter.35.cloned.1.call-done = bf16[16,3,64,512]{3,0,1,2:T(8,128)(2,1)} async-done(((bf16[16,3,1024,512]{3,0,1,2:T(8,128)(2,1)}), bf16[16,3,64,512]{3,0,1,2:T(8,128)(2,1)}) %reduce-scatter.35.cloned.1.call-update) | async-done | bytes 3145744
  2623.0 6.4 copy.104
  2629.5 629.6 %reduce-scatter.29.cloned.1.call-done = bf16[16,2048,64]{1,2,0:T(8,128)(2,1)} async-done(((bf16[16,2048,1024]{1,2,0:T(8,128)(2,1)}), bf16[16,2048,64]{1,2,0:T(8,128)(2,1)}) %reduce-scatter.29.cloned.1.call-update) | async-done | bytes 4194320 | tf_op jit(solution)/shard_map/reduce_scatter | solution.py:203
  3259.1 6.7 convert_element_type.154
  3265.7 1233.8 %reduce-scatter.37.cloned.1.call-done = bf16[16,2,64,2048]{3,0,1,2:T(8,128)(2,1)} async-done(((bf16[16,2,1024,2048]{3,0,1,2:T(8,128)(2,1)}), bf16[16,2,64,2048]{3,0,1,2:T(8,128)(2,1)}) %reduce-scatter.37.cloned.1.call-update) | async-done | bytes 8388624
  4499.5 14.4 copy.105
  (140 shorter events, 21.3 us)
Async XLA Ops:
  7.2 31.4 all-gather.9.cloned.1.call-start
  8.6 5.1 collective-permute-start
  13.7 0.6 copy-start.34
  13.9 1.0 copy-start.23
  14.3 444.0 %copy-start = (f32[16,16,1024]{2,0,1:T(8,128)}, f32[16,16,1024]{2,0,1:T(8,128)S(1)}, u32[]{:S(2)}) copy-start(f32[16,16,1024]{2,0,1:T(8,128)S(1)} %get-tuple-element.41) | copy-start | bytes 3145732
  14.3 0.7 copy-start.28
  16.0 272.1 %all-gather.11.cloned.1.call-start = ((), (), s32[]{:S(2)}) async-start(), calls=%async_computation.11 | async-start | bytes 53477376 | tf_op jit(solution)/shard_map/all_gather | solution.py:100
  16.8 398.0 %all-gather.13.cloned.1.call-start = ((), (), s32[]{:S(2)}) async-start(), calls=%async_computation.12 | async-start | bytes 17825792 | tf_op jit(solution)/shard_map/all_gather | solution.py:101
  17.5 440.9 %reduce-scatter.19.cloned.1.call-start = ((), (), s32[]{:S(2)}) async-start(), calls=%async_computation.13 | async-start | bytes 3145728 | tf_op jit(solution)/shard_map/reduce_scatter | solution.py:110
  319.5 1.2 copy-start.7
  427.0 33.8 copy-start.21
  427.0 56.2 %all-gather.15.cloned.1.call-start = ((), (), s32[]{:S(2)}) async-start(), calls=%async_computation.14 | async-start | bytes 1572864 | tf_op jit(solution)/shard_map/all_gather | solution.py:118
  459.8 1.0 copy-start.3
  459.8 1125.1 %copy-start.26 = (f32[16,16]{0,1:T(8,128)}, f32[16,16]{0,1:T(8,128)S(1)}, u32[]{:S(2)}) copy-start(f32[16,16]{0,1:T(8,128)S(1)} %add_rsqrt_fusion) | copy-start | bytes 3076
  461.8 1.0 copy-start.12
  461.8 665.6 %all-gather.17.cloned.1.call-start = ((), (), s32[]{:S(2)}) async-start(), calls=%async_computation.15 | async-start | bytes 142606336 | tf_op jit(solution)/shard_map/all_gather | solution.py:102
  462.4 714.4 %all-gather.21.cloned.1.call-start = ((), (), s32[]{:S(2)}) async-start(), calls=%async_computation.18 | async-start | bytes 1572864 | tf_op jit(solution)/shard_map/all_gather | solution.py:97
  463.9 1014.8 %all-gather.19.cloned.1.call-start = ((), (), s32[]{:S(2)}) async-start(), calls=%async_computation.16 | async-start | bytes 71303168 | tf_op jit(solution)/shard_map/all_gather | solution.py:103
  464.7 1118.6 %reduce-scatter.23.cloned.1.call-start = ((), (), s32[]{:S(2)}) async-start(), calls=%async_computation.19 | async-start | bytes 1572864 | tf_op jit(solution)/shard_map/reduce_scatter | solution.py:148
  1507.4 75.8 %copy-start.4 = (f32[16,16,1024]{2,0,1:T(8,128)S(1)}, f32[16,16,1024]{2,0,1:T(8,128)}, u32[]{:S(2)}) copy-start(f32[16,16,1024]{2,0,1:T(8,128)} %copy-done.3) | copy-start | bytes 3145732
  1563.5 44.8 all-gather.23.cloned.1.call-start
  1583.2 2.2 copy-start.13
  1583.2 2.2 copy-start.14
  1584.8 0.6 copy-start.31
  1586.8 97.9 %reduce-scatter.25.cloned.1.call-start = ((), (), s32[]{:S(2)}) async-start(), calls=%async_computation.21 | async-start | bytes 1572864 | tf_op jit(solution)/shard_map/reduce_scatter | solution.py:170
  1619.6 1.2 copy-start.8
  1622.5 1.2 copy-start.16
  1623.8 1.2 copy-start.17
  1629.2 1.0 copy-start.20
  1629.5 2.4 copy-start.19
  1632.8 22.3 copy-start.6
  1654.9 405.2 %reduce-scatter.21.cloned.1.call-start = ((), (), s32[]{:S(2)}) async-start(), calls=%async_computation.17 | async-start | bytes 1572864 | tf_op jit(solution)/shard_map/reduce_scatter | solution.py:126
  1683.5 1.2 copy-start.1
  1683.5 1.2 copy-start.24
  1683.5 1.2 copy-start.29
  1683.6 383.7 %reduce-scatter.33.cloned.1.call-start = ((), (), s32[]{:S(2)}) async-start(), calls=%async_computation.25 | async-start | bytes 540672
  1684.6 391.3 %reduce-scatter.31.cloned.1.call-start = ((), (), s32[]{:S(2)}) async-start(), calls=%async_computation.24 | async-start | bytes 540672
  1687.9 466.6 %reduce-scatter.27.cloned.1.call-start = ((), (), s32[]{:S(2)}) async-start(), calls=%async_computation.22 | async-start | bytes 17825792 | tf_op jit(solution)/shard_map/reduce_scatter | solution.py:197
  1700.1 1.2 copy-start.11
  1700.1 922.9 %reduce-scatter.35.cloned.1.call-start = ((), (), s32[]{:S(2)}) async-start(), calls=%async_computation.26 | async-start | bytes 53477376
  1785.5 1.2 copy-start.10
  1785.5 1473.6 %reduce-scatter.29.cloned.1.call-start = ((), (), s32[]{:S(2)}) async-start(), calls=%async_computation.23 | async-start | bytes 71303168 | tf_op jit(solution)/shard_map/reduce_scatter | solution.py:203
  1811.8 1.6 copy-start.9
  1811.8 1.9 copy-start.15
  1811.8 2687.7 %reduce-scatter.37.cloned.1.call-start = ((), (), s32[]{:S(2)}) async-start(), calls=%async_computation.27 | async-start | bytes 142606336
  2059.3 0.7 copy-start.36
  2059.3 0.8 copy-start.33
  2059.3 1.2 copy-start.2
  2059.3 1.6 copy-start.5
  2059.3 1.6 copy-start.22
  2059.3 1.5 copy-start.25
  2059.3 1.5 copy-start.27
  2059.4 1.5 copy-start.30
  2059.4 1.5 copy-start.32
  2060.1 3.9 copy-start.35
  2064.0 4.7 copy-start.18
  2064.2 10.3 collective-permute-start.1
Sparse Core Ops, SparseCore 0:
  16.1 22.3 all-gather.8
  40.1 247.9 all-gather.10
  290.3 124.3 all-gather.12
  427.1 31.1 reduce-scatter.18
  461.9 21.2 all-gather.14
  484.6 642.7 all-gather.16
  1129.5 20.7 all-gather.20
  1151.8 326.8 all-gather.18
  1563.6 19.6 reduce-scatter.22
  1586.9 21.2 all-gather.22
  1655.0 20.3 reduce-scatter.24
  1683.7 20.3 reduce-scatter.20
  1706.9 110.0 reduce-scatter.32
  1819.0 131.5 reduce-scatter.30
  1955.2 199.3 reduce-scatter.26
  2158.6 464.3 reduce-scatter.34
  2627.1 631.8 reduce-scatter.28
  3263.2 1236.3 reduce-scatter.36
where the time goes:
time: 4540 us; the launch traced here: 4520 us
  waiting for transfers between devices  3810 us (84%)
  matrix products  348 us (8%)
  local copies, waits for them, and re-layouts  315 us (7%)
    unnamed x22, waiting for transfers between devices  1700 us
    all_gather x1, waiting for transfers between devices, body(): lax.all_gather(w_gu, 'dp', axis=2, tiled=True)  644 us
    reduce_scatter x1, waiting for transfers between devices, body(): lax.psum_scatter(ffn_grads[1].astype(jnp.bfloat16), 'dp', scatter_dimensi...  630 us
    all_gather x1, waiting for transfers between devices, body(): lax.all_gather(w_down, 'dp', axis=2, tiled=True)  302 us
    all_gather x1, waiting for transfers between devices, body(): lax.all_gather(w_qkv, 'dp', axis=2, tiled=True)  250 us
    convert_element_type x1, local copies, waits for them, and re-layouts, body(): ffn_grads[0].astype(jnp.bfloat16)  193 us
  transfers between devices with their start and end apart: 20, of which 14 were waited for; matrix products, arithmetic and copies ran while one was open for 11% of the time, Pallas kernels for 0%

commit v1 on v0

v1 whole, which is shorter than its diff:
```python
import jax
import jax.numpy as jnp
from jax import lax
from jax.sharding import PartitionSpec as P

HD = 64


norm_eps = 1e-06


def from_behind(value, axis, steps):
    count = lax.axis_size(axis)
    initial, last = (max(0, -steps), min(count, count - steps))
    return lax.ppermute(value, axis, [(source, source + steps) for source in range(initial, last)])


def delayed(frames, offsets):
    prior = from_behind(frames[-2:], ("dp", "mp"), 1)
    joined = jnp.concatenate([prior, frames], axis=0).astype(jnp.float32)
    row_count = frames.shape[0]
    return jnp.where((offsets == 1)[:, :, None], joined[1 : row_count + 1], joined[0:row_count])


def normalize(residual, norm_gain):
    scaling = lax.rsqrt(jnp.mean(residual * residual, axis=-1, keepdims=True) + norm_eps)
    unit_rows = residual * scaling
    return (unit_rows, scaling, (unit_rows * norm_gain).astype(jnp.bfloat16))


def norm_back(grad_normed, unit_rows, scaling, norm_gain):
    weighted = grad_normed * norm_gain
    inner_mean = jnp.mean(weighted * unit_rows, axis=-1, keepdims=True)
    return (scaling * (weighted - unit_rows * inner_mean), jnp.sum(grad_normed * unit_rows, axis=0))


def head_scores(qkv_low, head_width):
    frame_count = qkv_low.shape[0]
    positions = qkv_low.shape[1]
    head_count = qkv_low.shape[3] // head_width
    queries = qkv_low[:, :, 0].reshape(frame_count, positions, head_count, head_width)
    key_rows = qkv_low[:, :, 1].reshape(frame_count, positions, head_count, head_width)
    value_rows = qkv_low[:, :, 2].reshape(frame_count, positions, head_count, head_width)
    scaling = head_width ** (-0.5)
    scores = (
        jnp.einsum("fphe,fqhe->fhpq", queries, key_rows, preferred_element_type=jnp.float32)
        * scaling
    )
    causal = jnp.arange(positions)[:, None] >= jnp.arange(positions)[None, :]
    scores = jnp.where(causal, scores, -1e30)
    return (queries, key_rows, value_rows, scores, scaling)


def attend(qkv_low, head_width):
    queries, key_rows, value_rows, scores, scaling = head_scores(qkv_low, head_width)
    row_max = jnp.max(scores, axis=-1, keepdims=True)
    log_total = row_max + jnp.log(jnp.sum(jnp.exp(scores - row_max), axis=-1, keepdims=True))
    probs_low = jnp.exp(scores - log_total).astype(jnp.bfloat16)
    mixed = jnp.einsum("fhpq,fqhe->fphe", probs_low, value_rows, preferred_element_type=jnp.float32)
    mixed_low = mixed.reshape(qkv_low.shape[0], qkv_low.shape[1], qkv_low.shape[3]).astype(
        jnp.bfloat16
    )
    return (mixed_low, log_total)


def attend_back(qkv_low, grad_mixed, log_total, head_width):
    queries, key_rows, value_rows, scores, scaling = head_scores(qkv_low, head_width)
    attn_probs = jnp.exp(scores - log_total)
    probs_low = attn_probs.astype(jnp.bfloat16)
    grad_heads = grad_mixed.reshape(queries.shape)
    grad_values = jnp.einsum(
        "fhpq,fphe->fqhe", probs_low, grad_heads, preferred_element_type=jnp.float32
    )
    grad_probs = jnp.einsum(
        "fphe,fqhe->fhpq", grad_heads, value_rows, preferred_element_type=jnp.float32
    )
    row_inner = jnp.sum(attn_probs * grad_probs, axis=-1, keepdims=True)
    grad_scores = (attn_probs * (grad_probs - row_inner)).astype(jnp.bfloat16)
    grad_queries = (
        jnp.einsum("fhpq,fqhe->fphe", grad_scores, key_rows, preferred_element_type=jnp.float32)
        * scaling
    )
    grad_keys = (
        jnp.einsum("fhpq,fphe->fqhe", grad_scores, queries, preferred_element_type=jnp.float32)
        * scaling
    )
    stacked = jnp.stack([grad_queries, grad_keys, grad_values], axis=2)
    return stacked.reshape(qkv_low.shape).astype(jnp.bfloat16)


def swap(value):
    return lax.all_to_all(value, "dp", split_axis=0, concat_axis=0, tiled=True)


def weights_to_positions(shards):
    copies = lax.axis_size("dp") // shards.shape[0]
    return swap(jnp.repeat(shards, copies, axis=0) if copies > 1 else shards)


def grads_to_shards(blocks, positions):
    arrived = swap(blocks.astype(jnp.bfloat16))
    copies = arrived.shape[0] // positions
    parts = arrived.reshape(positions, copies, *arrived.shape[1:]).astype(jnp.float32)
    return jnp.sum(parts, axis=1) if copies > 1 else parts[:, 0]


def rows_to_positions(value):
    frame_count, positions, width = value.shape
    count = lax.axis_size("dp")
    copies = count // positions
    part = frame_count // copies
    split = value.reshape(copies, part, positions, width).transpose(2, 0, 1, 3)
    return swap(split.reshape(count, part, width))


def rows_to_frames(value, positions):
    arrived = swap(value)
    count, part, width = arrived.shape
    copies = count // positions
    split = arrived.reshape(positions, copies, part, width).transpose(1, 2, 0, 3)
    return split.reshape(copies * part, positions, width)


def both(value):
    return lax.all_gather(value, "mp", axis=0, tiled=True)


def matmul(left, right, spec):
    return jnp.einsum(spec, left, right, preferred_element_type=jnp.float32)


def body(frames, offsets, gain_attn, w_qkv, w_out, gain_ffn, w_gu, w_down, cotangent):
    row_count, positions, width = frames.shape
    count = lax.axis_size("dp")
    groups = lax.axis_size("mp")
    copies = count // positions
    part = row_count // copies
    mine = lax.axis_index("dp") // copies
    attn_gain = lax.dynamic_index_in_dim(gain_attn, mine, 0, keepdims=False)
    ffn_gain = lax.dynamic_index_in_dim(gain_ffn, mine, 0, keepdims=False)
    heads_width = w_qkv.shape[3]
    units = w_gu.shape[3]

    def flat(value):
        return value.reshape(-1, value.shape[-1])

    def own_sum(value):
        return lax.psum_scatter(
            value.reshape(groups * count, part, width), "mp", scatter_dimension=0, tiled=True
        ).astype(jnp.float32)

    def to_heads(value):
        split = value.reshape(groups, count, part, -1).transpose(1, 0, 2, 3)
        return rows_to_frames(split.reshape(count, groups * part, -1), positions)

    resid_bf = delayed(frames, offsets).astype(jnp.bfloat16)
    resid_in = rows_to_positions(resid_bf).astype(jnp.float32)
    cot_own = rows_to_positions(cotangent)
    unit_one, scale_one, normed_one = normalize(resid_in, attn_gain)
    group_norm = flat(both(normed_one))
    group_cot = flat(both(cot_own))
    full_qkv = weights_to_positions(w_qkv).transpose(1, 0, 2, 3).reshape(3, width, heads_width)
    full_out = weights_to_positions(w_out.transpose(0, 2, 1)).reshape(width, heads_width)
    full_gu = weights_to_positions(w_gu).transpose(1, 0, 2, 3).reshape(2, width, units)
    full_down = weights_to_positions(w_down.transpose(0, 2, 1)).reshape(width, units)

    qkv_pos = matmul(group_norm, full_qkv, "xd,jde->xje").astype(jnp.bfloat16)
    qkv_low = to_heads(qkv_pos).reshape(copies * groups * part, positions, 3, heads_width)
    mixed_low, log_total = attend(qkv_low, HD)

    def frames_to_rows(value):
        moved = rows_to_positions(value)
        split = moved.reshape(count, groups, part, -1).transpose(1, 0, 2, 3)
        return split.reshape(groups * count * part, -1)

    mixed_pos = frames_to_rows(mixed_low)
    attn_sum = own_sum(matmul(mixed_pos, full_out, "xe,de->xd"))
    hidden_in = resid_in + attn_sum
    unit_two, scale_two, normed_two = normalize(hidden_in, ffn_gain)
    group_two = flat(both(normed_two))
    gate_up = matmul(group_two, full_gu, "xd,jde->jxe")
    gate_pre = gate_up[0]
    up_pre = gate_up[1]
    sigmoid_gate = jax.nn.sigmoid(gate_pre)
    silu_gate = gate_pre * sigmoid_gate
    hidden_low = (silu_gate * up_pre).astype(jnp.bfloat16)
    ffn_sum = own_sum(matmul(hidden_low, full_down, "xe,de->xd").astype(jnp.bfloat16))
    result = rows_to_frames((hidden_in + ffn_sum).astype(jnp.bfloat16), positions)

    grad_down = matmul(group_cot, hidden_low, "xd,xe->de")
    grad_hidden = matmul(group_cot, full_down, "xd,de->xe")
    slope = sigmoid_gate * (1.0 + gate_pre * (1.0 - sigmoid_gate))
    grad_gu = jnp.stack([grad_hidden * up_pre * slope, grad_hidden * silu_gate]).astype(
        jnp.bfloat16
    )
    grad_wgu = matmul(group_two, grad_gu, "xd,jxe->jde")
    grad_normed_two = own_sum(matmul(grad_gu, full_gu, "jxe,jde->xd").astype(jnp.bfloat16))
    back_two, gain_two = norm_back(grad_normed_two, unit_two, scale_two, ffn_gain)
    grad_hidden_in = cot_own.astype(jnp.float32) + back_two
    group_grad = flat(both(grad_hidden_in.astype(jnp.bfloat16)))
    grad_wout = matmul(group_grad, mixed_pos, "xd,xe->de")
    grad_mixed = matmul(group_grad, full_out, "xd,de->xe").astype(jnp.bfloat16)
    grad_mixed_low = to_heads(grad_mixed)
    grad_qkv_low = attend_back(qkv_low, grad_mixed_low, log_total, HD)
    grad_qkv = frames_to_rows(
        grad_qkv_low.reshape(copies * groups * part, positions, 3 * heads_width)
    ).reshape(-1, 3, heads_width)
    grad_wqkv = matmul(group_norm, grad_qkv, "xd,xje->jde")
    grad_normed_one = own_sum(matmul(grad_qkv, full_qkv, "xje,jde->xd").astype(jnp.bfloat16))
    back_one, gain_one = norm_back(grad_normed_one, unit_one, scale_one, attn_gain)
    grad_resid = rows_to_frames((grad_hidden_in + back_one).astype(jnp.bfloat16), positions).astype(
        jnp.float32
    )
    one_step = jnp.where((offsets == 1)[:, :, None], grad_resid, 0.0)
    two_step = jnp.where((offsets == 2)[:, :, None], grad_resid, 0.0)
    spread = jnp.pad(one_step, ((1, 1), (0, 0), (0, 0))) + jnp.pad(
        two_step, ((0, 2), (0, 0), (0, 0))
    )
    returned = from_behind(spread[:2].astype(jnp.bfloat16), ("dp", "mp"), -1).astype(jnp.float32)
    grad_frames = (spread[2:] + jnp.pad(returned, ((row_count - 2, 0), (0, 0), (0, 0)))).astype(
        jnp.bfloat16
    )
    gains = jnp.stack([jnp.sum(gain_one, axis=0), jnp.sum(gain_two, axis=0)])
    gains = gains.reshape(2, count, groups, width // (count * groups))
    gains = lax.psum_scatter(
        gains.transpose(2, 1, 0, 3), "mp", scatter_dimension=0, tiled=False
    )
    gains = swap(gains)
    gains = jnp.sum(gains.reshape(positions, copies, 2, -1), axis=1)

    def split_rows(value):
        stacked = value.shape[0]
        return value.reshape(stacked, count, width // count, -1).transpose(1, 0, 2, 3)

    shard_qkv = grads_to_shards(split_rows(grad_wqkv), positions)
    shard_out = grads_to_shards(grad_wout.reshape(count, -1, heads_width), positions)
    shard_gu = grads_to_shards(split_rows(grad_wgu), positions)
    shard_down = grads_to_shards(grad_down.reshape(count, -1, units), positions)
    return (
        result,
        grad_frames,
        gains[:, 0],
        shard_qkv,
        shard_out.transpose(0, 2, 1),
        gains[:, 1],
        shard_gu,
        shard_down.transpose(0, 2, 1),
    )


def solution(mesh):
    return jax.shard_map(
        body,
        mesh=mesh,
        in_specs=(
            P(("dp", "mp"), None, None),
            P(("dp", "mp"), None),
            P(),
            P(None, None, "dp", "mp"),
            P(None, "mp", "dp"),
            P(),
            P(None, None, "dp", "mp"),
            P(None, "mp", "dp"),
            P(("dp", "mp"), None, None),
        ),
        out_specs=(
            P(("dp", "mp"), None, None),
            P(("dp", "mp"), None, None),
            P(None, ("dp", "mp")),
            P(None, None, "dp", "mp"),
            P(None, "mp", "dp"),
            P(None, ("dp", "mp")),
            P(None, None, "dp", "mp"),
            P(None, "mp", "dp"),
        ),
        check_vma=False,
    )
```

time: 4540 us -> 1100 us (0.24)
  waiting for transfers between devices: 3810 us -> 500 us
  blocking collectives: 0 us -> 290 us
  matrix products: 348 us -> 78.7 us
  local copies, waits for them, and re-layouts: 315 us -> 97.1 us
  starting transfers between devices: 8.46 us -> 70.7 us
    unnamed x22 -> x9, waiting for transfers between devices: 1700 us -> 0.65 us
    all_gather x8 -> x4, waiting for transfers between devices: 1350 us -> 44.9 us  [both(): return lax.all_gather(value, 'mp', axis=0, tiled=True)]
    reduce_scatter x6 -> x5, waiting for transfers between devices: 758 us -> 72.8 us  [the longest x4 68.7 us: own_sum(): lax.psum_scatter(value.reshape(groups * count, part, width), 'mp', scatte...]
    all_to_all x0 -> x5, blocking collectives: none -> 290 us  [swap(): return lax.all_to_all(value, 'dp', split_axis=0, concat_axis=0, tiled=True)]
    dot_general x12, matrix products: 339 us -> 69.5 us  [matmul(): return jnp.einsum(spec, left, right, preferred_element_type=jnp.float32)]
    convert_element_type x2 -> x5, local copies, waits for them, and re-layouts: 255 us -> 18 us  [the longest x3 13.5 us: grads_to_shards(): arrived = swap(blocks.astype(jnp.bfloat16))]
    all_to_all x0 -> x12, waiting for transfers between devices: none -> 213 us  [swap(): return lax.all_to_all(value, 'dp', split_axis=0, concat_axis=0, tiled=True)]
    ppermute x2, waiting for transfers between devices: 4.76 us -> 168 us  [from_behind(): lax.ppermute(value, axis, [(source, source + steps) for source in range(i...]
  transfers between devices with their start and end apart: 20 -> 23, of which waited for: 14 -> 17; matrix products, arithmetic and copies ran while one was open for 11% -> 17% of each run, Pallas kernels for 0% -> 0%
where the time goes in v1:
time: 1100 us
  waiting for transfers between devices  500 us (45%)
  blocking collectives  290 us (26%)
  local copies, waits for them, and re-layouts  97.1 us (9%)
  matrix products  78.7 us (7%)
  starting transfers between devices  70.7 us (6%)
  other arithmetic  46.6 us (4%)
  between operations  14.6 us (1%)
    all_to_all x5, blocking collectives, swap(): return lax.all_to_all(value, 'dp', split_axis=0, concat_axis=0, tiled=True)  290 us
    all_to_all x12, waiting for transfers between devices, swap(): return lax.all_to_all(value, 'dp', split_axis=0, concat_axis=0, tiled=True)  213 us
    ppermute x2, waiting for transfers between devices, from_behind(): lax.ppermute(value, axis, [(source, source + steps) for source in range(i...  168 us
    dot_general x12, matrix products, matmul(): return jnp.einsum(spec, left, right, preferred_element_type=jnp.float32)  69.5 us
    reduce_scatter x4, waiting for transfers between devices, own_sum(): lax.psum_scatter(value.reshape(groups * count, part, width), 'mp', scatte...  68.7 us
    all_to_all x12, starting transfers between devices, swap(): return lax.all_to_all(value, 'dp', split_axis=0, concat_axis=0, tiled=True)  62.6 us
    all_gather x4, waiting for transfers between devices, both(): return lax.all_gather(value, 'mp', axis=0, tiled=True)  44.9 us
  transfers between devices with their start and end apart: 23, of which 17 were waited for; matrix products, arithmetic and copies ran while one was open for 17% of the time, Pallas kernels for 0%

profile of v1, /device:TPU:15, one launch (start us, length us, event | category | flops | bytes accessed | tf_op | source)
XLA Modules:
  0.0 1097.2 jit_solution(1269253977912668090)
XLA Ops:
  8.6 3.7 collective-permute-start
  14.1 21.0 %all_to_all.85 = bf16[16,16,1024]{2,1,0:T(8,128)(2,1)S(1)} all-to-all(bf16[16,16,1024]{2,1,0:T(8,128)(2,1)S(1)} %fusion.54), channel_id=1, replica_groups=mesh['dp'=16,'mp'=2] {'dp'}, dimensions={0} | all-to-all | bytes 1048576 | tf_op jit(solution)/shard_map/all_to_all | solution.py:92
  35.1 5.0 all-to-all-start.1
  42.6 67.6 %all-to-all-done.1 = bf16[16,3,64,512]{3,2,1,0:T(8,128)(2,1)} async-done(((bf16[16,3,64,512]{3,2,1,0:T(8,128)(2,1)}), bf16[16,3,64,512]{3,2,1,0:T(8,128)(2,1)}, u32[]{:S(2)}, u32[]{:S(2)}) %all-to-all-start.1) | async-done | bytes 3145760 | tf_op jit(solution)/shard_map/all_to_all | solution.py:92
  110.2 4.8 all-to-all-start.8
  114.9 3.9 copy.76
  118.8 4.0 convolution_convert_fusion.2
  124.2 3.1 reshape.217
  128.8 42.0 %all_to_all.86 = bf16[16,32,1536]{2,1,0:T(8,128)(2,1)} all-to-all(bf16[16,32,1536]{2,1,0:T(8,128)(2,1)S(1)} %bitcast.212), channel_id=1, replica_groups=mesh['dp'=16,'mp'=2] {'dp'}, dimensions={0} | all-to-all | bytes 3145728 | tf_op jit(solution)/shard_map/all_to_all | solution.py:92
  170.8 5.5 all-to-all-start.4
  178.4 4.6 reshape_reshape.10
  183.0 7.6 slice_reduce_fusion.1
  192.3 2.6 reshape_squeeze.14
  203.2 19.4 %all_to_all.87 = bf16[16,32,512]{2,1,0:T(8,128)(2,1)S(1)} all-to-all(bf16[16,32,512]{2,1,0:T(8,128)(2,1)S(1)} %copy.85), channel_id=1, replica_groups=mesh['dp'=16,'mp'=2] {'dp'}, dimensions={0} | all-to-all | bytes 1048576 | tf_op jit(solution)/shard_map/all_to_all | solution.py:92
  222.6 187.5 %all_to_all.88 = bf16[16,2,64,2048]{3,2,1,0:T(8,128)(2,1)} all-to-all(bf16[16,2,64,2048]{3,2,1,0:T(8,128)(2,1)} %param.15), channel_id=1, replica_groups=mesh['dp'=16,'mp'=2] {'dp'}, dimensions={0} | all-to-all | bytes 16777216 | tf_op jit(solution)/shard_map/all_to_all | solution.py:92
  410.1 5.0 all-to-all-start.6
  415.2 3.5 fusion.63
  420.1 30.1 %reduce-scatter.6.cloned.1.call-done = f32[16,16,1024]{2,1,0:T(8,128)} async-done(((f32[32,16,1024]{2,1,0:T(8,128)}), f32[16,16,1024]{2,1,0:T(8,128)}) %reduce-scatter.6.cloned.1.call-update) | async-done | bytes 1048592 | tf_op jit(solution)/shard_map/reduce_scatter | solution.py:148
  453.4 8.4 copy.87
  461.9 12.4 %all-gather.7.cloned.1.call-done = bf16[32,16,1024]{2,1,0:T(8,128)(2,1)} async-done(((bf16[16,16,1024]{2,1,0:T(8,128)(2,1)}), bf16[32,16,1024]{2,1,0:T(8,128)(2,1)}) %all-gather.7.cloned.1.call-update) | async-done | bytes 1048592 | tf_op jit(solution)/shard_map/all_gather | solution.py:125
  474.2 11.6 %convolution_bitcast_fusion = f32[2,512,2048]{2,1,0:T(8,128)} fusion(bf16[512,1024,1]{1,0,2:T(8,128)(2,1)} %bitcast.227, bf16[2,1024,2048]{2,1,0:T(8,128)(2,1)} %bitcast.205), kind=kOutput, calls=%fused_computation.3 | convolution fusion | flops 4294967296 | bytes 17825792 | tf_op jit(solution)/shard_map/xd,jde->jxe/dot_general | solution.py:129
  485.9 11.1 %all-gather.9.cloned.1.call-done = bf16[32,16,1024]{2,1,0:T(8,128)(2,1)} async-done(((bf16[16,16,1024]{2,1,0:T(8,128)(2,1)}), bf16[32,16,1024]{2,1,0:T(8,128)(2,1)}) %all-gather.9.cloned.1.call-update) | async-done | bytes 1048592 | tf_op jit(solution)/shard_map/all_gather | solution.py:125
  496.9 10.6 all-to-all-done.6
  507.5 8.6 fusion.14
  516.2 5.5 bitcast_convert_fusion.1
  522.0 18.6 %reduce-scatter.10.cloned.1.call-done = bf16[16,16,1024]{2,1,0:T(8,128)(2,1)} async-done(((bf16[32,16,1024]{2,1,0:T(8,128)(2,1)}), bf16[16,16,1024]{2,1,0:T(8,128)(2,1)}) %reduce-scatter.10.cloned.1.call-update) | async-done | bytes 524304 | tf_op jit(solution)/shard_map/reduce_scatter | solution.py:148
  544.4 21.4 %all-gather.11.cloned.1.call-done = bf16[32,16,1024]{2,1,0:T(8,128)(2,1)} async-done(((bf16[16,16,1024]{2,1,0:T(8,128)(2,1)}), bf16[32,16,1024]{2,1,0:T(8,128)(2,1)}) %all-gather.11.cloned.1.call-update) | async-done | bytes 1048592 | tf_op jit(solution)/shard_map/all_gather | solution.py:125
  568.9 6.5 all-to-all-start.9
  577.7 3.0 convolution_convert_fusion.5
  580.7 8.4 all-to-all-done.9
  589.1 4.9 all-to-all-start.14
  602.3 2.8 multiply_reduce_fusion
  616.2 3.1 convert_element_type.185
  619.4 3.4 copy.101
  622.8 6.4 all-to-all-start.10
  629.2 4.8 multiply_convert_fusion
  635.2 4.4 convolution_convert_fusion.1
  639.7 25.5 %all-to-all-done.10 = bf16[16,32,1536]{2,1,0:T(8,128)(2,1)S(1)} async-done(((bf16[16,32,1536]{2,1,0:T(8,128)(2,1)}), bf16[16,32,1536]{2,1,0:T(8,128)(2,1)S(1)}, u32[]{:S(2)}, u32[]{:S(2)}) %all-to-all-start.10) | async-done | bytes 1572896 | tf_op jit(solution)/shard_map/all_to_all | solution.py:92
  665.2 4.8 all-to-all-start.16
  671.3 4.6 reshape_reshape.12
  675.9 2.8 copy.107
  678.7 5.2 bitcast_convert_fusion
  684.1 19.9 %reduce-scatter.12.cloned.1.call-done = bf16[16,16,1024]{2,1,0:T(8,128)(2,1)} async-done(((bf16[32,16,1024]{2,1,0:T(8,128)(2,1)}), bf16[16,16,1024]{2,1,0:T(8,128)(2,1)}) %reduce-scatter.12.cloned.1.call-update) | async-done | bytes 524304 | tf_op jit(solution)/shard_map/reduce_scatter | solution.py:148
  706.3 6.3 fusion.20
  712.6 4.1 reduce-scatter.14.cloned.1.call-done
  718.0 44.5 %all-to-all-done.16 = bf16[16,64,2048]{2,1,0:T(8,128)(2,1)} async-done(((bf16[16,64,2048]{2,1,0:T(8,128)(2,1)}), bf16[16,64,2048]{2,1,0:T(8,128)(2,1)}, u32[]{:S(2)}, u32[]{:S(2)}) %all-to-all-start.16) | async-done | bytes 4194336 | tf_op jit(solution)/shard_map/all_to_all | solution.py:92
  762.5 4.8 all-to-all-start.12
  767.3 2.6 fusion.32
  771.4 20.1 %all_to_all.89 = bf16[16,16,1024]{2,1,0:T(8,128)(2,1)} all-to-all(bf16[16,16,1024]{2,1,0:T(8,128)(2,1)} %get-tuple-element.44), channel_id=1, replica_groups=mesh['dp'=16,'mp'=2] {'dp'}, dimensions={0} | all-to-all | bytes 1048576 | tf_op jit(solution)/shard_map/all_to_all | solution.py:92
  791.5 5.4 all-to-all-start.11
  796.9 4.7 convert_bitcast_fusion.1
  801.6 3.2 copy.108
  806.7 3.8 all-to-all-done.11
  810.4 4.8 all-to-all-start.13
  815.3 10.4 convolution_convert_fusion
  825.7 8.4 copy.149
  834.1 51.0 %all-to-all-done.13 = bf16[16,3,64,512]{3,2,1,0:T(8,128)(2,1)S(1)} async-done(((bf16[16,3,64,512]{3,2,1,0:T(8,128)(2,1)}), bf16[16,3,64,512]{3,2,1,0:T(8,128)(2,1)S(1)}, u32[]{:S(2)}, u32[]{:S(2)}) %all-to-all-start.13) | async-done | bytes 3145760 | tf_op jit(solution)/shard_map/all_to_all | solution.py:92
  885.1 4.8 all-to-all-start.15
  890.0 2.8 convert_bitcast_fusion.2
  892.8 6.7 convert_bitcast_fusion
  900.9 3.3 collective-permute-start.1
  905.9 167.9 %collective-permute-done.1 = bf16[2,16,1024]{2,0,1:T(2,128)(2,1)S(1)} collective-permute-done((bf16[2,16,1024]{2,0,1:T(2,128)(2,1)S(1)}, bf16[2,16,1024]{2,0,1:T(2,128)(2,1)S(1)}, u32[]{:S(2)}, u32[]{:S(2)}) %collective-permute-start.1) | collective-permute-done | bytes 65568 | tf_op jit(solution)/shard_map/ppermute | solution.py:15
  1075.3 3.6 convert_element_type.198
  1078.8 11.7 %convert_element_type.204 = f32[16,2,64,2048]{3,2,1,0:T(8,128)} convert(bf16[16,2,64,2048]{3,2,1,0:T(8,128)(2,1)} %all-to-all-done.15) | non-fusion elementwise | flops 4194304 | bytes 25165824 | tf_op jit(solution)/shard_map/convert_element_type | solution.py:103
  (142 shorter events, 68.2 us)
Async XLA Ops:
  7.2 33.1 %copy-start = (f32[16,1024]{1,0:T(8,128)S(1)}, f32[16,1024]{1,0:T(8,128)}, u32[]{:S(2)}) copy-start(f32[16,1024]{1,0:T(8,128)} %param.11) | copy-start | bytes 196612
  8.6 5.0 collective-permute-start
  35.1 5.3 copy-start.3
  35.1 75.1 %all-to-all-start.1 = ((bf16[16,3,64,512]{3,2,1,0:T(8,128)(2,1)}), bf16[16,3,64,512]{3,2,1,0:T(8,128)(2,1)}, u32[]{:S(2)}, u32[]{:S(2)}) async-start(bf16[16,3,64,512]{3,2,1,0:T(8,128)(2,1)} %param.12), calls=%async_computation.1 | async-start | bytes 6291456 | tf_op jit(solution)/shard_map/all_to_all | solution.py:92
  40.2 1.3 copy-start.22
  40.2 78.6 %all-gather.5.cloned.1.call-start = ((), (), s32[]{:S(2)}) async-start(), calls=%async_computation.22 | async-start | bytes 1572864 | tf_op jit(solution)/shard_map/all_gather | solution.py:125
  110.2 18.6 %all-to-all-start.8 = ((bf16[16,16,1024]{2,1,0:T(8,128)(2,1)}), bf16[16,16,1024]{2,1,0:T(8,128)(2,1)S(1)}, u32[]{:S(2)}, u32[]{:S(2)}) async-start(bf16[16,16,1024]{2,1,0:T(8,128)(2,1)} %bitcast.204), calls=%async_computation.10 | async-start | bytes 1048576 | tf_op jit(solution)/shard_map/all_to_all | solution.py:92
  128.8 42.0 %copy-start.8 = (bf16[16,16,1024]{2,1,0:T(8,128)(2,1)}, bf16[16,16,1024]{2,1,0:T(8,128)(2,1)S(1)}, u32[]{:S(2)}) copy-start(bf16[16,16,1024]{2,1,0:T(8,128)(2,1)S(1)} %all-to-all-done.8) | copy-start | bytes 1572868
  170.8 5.6 copy-start.10
  170.8 32.4 %all-to-all-start.4 = ((bf16[16,64,512]{2,1,0:T(8,128)(2,1)}), bf16[16,64,512]{2,1,0:T(8,128)(2,1)}, u32[]{:S(2)}, u32[]{:S(2)}) async-start(bf16[16,64,512]{2,1,0:T(8,128)(2,1)} %bitcast.229), calls=%async_computation.4 | async-start | bytes 2097152 | tf_op jit(solution)/shard_map/all_to_all | solution.py:92
  190.6 4.4 copy-start.15
  192.3 7.3 copy-start.7
  410.1 97.5 %all-to-all-start.6 = ((bf16[16,64,2048]{2,1,0:T(8,128)(2,1)}), bf16[16,64,2048]{2,1,0:T(8,128)(2,1)}, u32[]{:S(2)}, u32[]{:S(2)}) async-start(bf16[16,64,2048]{2,1,0:T(8,128)(2,1)} %bitcast.217), calls=%async_computation.7 | async-start | bytes 8388608 | tf_op jit(solution)/shard_map/all_to_all | solution.py:92
  415.1 35.2 %reduce-scatter.6.cloned.1.call-start = ((), (), s32[]{:S(2)}) async-start(), calls=%async_computation.23 | async-start | bytes 3145728 | tf_op jit(solution)/shard_map/reduce_scatter | solution.py:148
  415.2 3.5 copy-start.16
  418.7 55.6 %all-gather.7.cloned.1.call-start = ((), (), s32[]{:S(2)}) async-start(), calls=%async_computation.24 | async-start | bytes 1572864 | tf_op jit(solution)/shard_map/all_gather | solution.py:125
  452.8 44.2 %all-gather.9.cloned.1.call-start = ((), (), s32[]{:S(2)}) async-start(), calls=%async_computation.26 | async-start | bytes 1572864 | tf_op jit(solution)/shard_map/all_gather | solution.py:125
  453.4 87.2 %reduce-scatter.10.cloned.1.call-start = ((), (), s32[]{:S(2)}) async-start(), calls=%async_computation.27 | async-start | bytes 1572864 | tf_op jit(solution)/shard_map/reduce_scatter | solution.py:148
  507.5 8.6 copy-start.2
  516.1 5.6 copy-start.24
  516.1 5.6 copy-start.25
  521.7 44.1 %all-gather.11.cloned.1.call-start = ((), (), s32[]{:S(2)}) async-start(), calls=%async_computation.28 | async-start | bytes 1572864 | tf_op jit(solution)/shard_map/all_gather | solution.py:125
  568.9 20.2 %all-to-all-start.9 = ((bf16[16,32,512]{2,1,0:T(8,128)(2,1)}), bf16[16,32,512]{2,1,0:T(8,128)(2,1)}, u32[]{:S(2)}, u32[]{:S(2)}) async-start(bf16[16,32,512]{2,1,0:T(8,128)(2,1)} %bitcast.225), calls=%async_computation.12 | async-start | bytes 1048576 | tf_op jit(solution)/shard_map/all_to_all | solution.py:92
  589.1 33.7 %all-to-all-start.14 = ((bf16[16,64,512]{2,1,0:T(8,128)(2,1)}), bf16[16,64,512]{2,1,0:T(8,128)(2,1)}, u32[]{:S(2)}, u32[]{:S(2)}) async-start(bf16[16,64,512]{2,1,0:T(8,128)(2,1)} %convolution_convert_fusion.5), calls=%async_computation.19 | async-start | bytes 2097152 | tf_op jit(solution)/shard_map/all_to_all | solution.py:92
  605.1 1.6 copy-start.13
  605.8 1.0 copy-start.5
  607.4 3.8 copy-start.6
  607.5 3.8 copy-start.12
  611.8 1.7 copy-start.19
  611.8 1.7 copy-start.20
  622.8 42.4 %all-to-all-start.10 = ((bf16[16,32,1536]{2,1,0:T(8,128)(2,1)}), bf16[16,32,1536]{2,1,0:T(8,128)(2,1)S(1)}, u32[]{:S(2)}, u32[]{:S(2)}) async-start(bf16[16,32,1536]{2,1,0:T(8,128)(2,1)} %copy.101), calls=%async_computation.13 | async-start | bytes 3145728 | tf_op jit(solution)/shard_map/all_to_all | solution.py:92
  629.1 6.1 copy-start.23
  633.9 1.3 copy-start.14
  665.2 97.2 %all-to-all-start.16 = ((bf16[16,64,2048]{2,1,0:T(8,128)(2,1)}), bf16[16,64,2048]{2,1,0:T(8,128)(2,1)}, u32[]{:S(2)}, u32[]{:S(2)}) async-start(bf16[16,64,2048]{2,1,0:T(8,128)(2,1)} %bitcast.218), calls=%async_computation.21 | async-start | bytes 8388608 | tf_op jit(solution)/shard_map/all_to_all | solution.py:92
  670.0 34.0 %reduce-scatter.12.cloned.1.call-start = ((), (), s32[]{:S(2)}) async-start(), calls=%async_computation.29 | async-start | bytes 1572864 | tf_op jit(solution)/shard_map/reduce_scatter | solution.py:148
  678.7 25.3 %copy-start.4 = (bf16[16,16,1024]{2,1,0:T(8,128)(2,1)S(1)}, bf16[16,16,1024]{2,1,0:T(8,128)(2,1)}, u32[]{:S(2)}) copy-start(bf16[16,16,1024]{2,1,0:T(8,128)(2,1)} %copy-done.3) | copy-start | bytes 1572868
  683.9 32.7 %reduce-scatter.14.cloned.1.call-start = ((), (), s32[]{:S(2)}) async-start(), calls=%async_computation.30 | async-start | bytes 49152 | tf_op jit(solution)/shard_map/reduce_scatter | solution.py:225
  706.2 61.0 %copy-start.9 = (bf16[16,16,1024]{2,1,0:T(8,128)(2,1)S(1)}, bf16[16,16,1024]{2,1,0:T(8,128)(2,1)}, u32[]{:S(2)}) copy-start(bf16[16,16,1024]{2,1,0:T(8,128)(2,1)} %copy-done.8) | copy-start | bytes 1572868
  706.3 61.0 %copy-start.11 = (bf16[16,16,1024]{2,1,0:T(8,128)(2,1)S(1)}, bf16[16,16,1024]{2,1,0:T(8,128)(2,1)}, u32[]{:S(2)}) copy-start(bf16[16,16,1024]{2,1,0:T(8,128)(2,1)} %reduce-scatter.10.cloned.1.call-done) | copy-start | bytes 1572868
  706.3 61.0 %copy-start.17 = (bf16[16,16,1024]{2,1,0:T(8,128)(2,1)S(1)}, bf16[16,16,1024]{2,1,0:T(8,128)(2,1)}, u32[]{:S(2)}) copy-start(bf16[16,16,1024]{2,1,0:T(8,128)(2,1)} %reduce-scatter.12.cloned.1.call-done) | copy-start | bytes 1572868
  706.3 61.0 %reduce-scatter.8.cloned.1.call-start = ((), (), s32[]{:S(2)}) async-start(), calls=%async_computation.25 | async-start | bytes 1572864 | tf_op jit(solution)/shard_map/reduce_scatter | solution.py:148
  762.5 8.9 all-to-all-start.12
  769.9 27.0 %copy-start.21 = (bf16[512,3,512]{0,2,1:T(8,128)(2,1)S(1)}, bf16[512,3,512]{0,2,1:T(8,128)(2,1)}, u32[]{:S(2)}) copy-start(bf16[512,3,512]{0,2,1:T(8,128)(2,1)} %copy.107) | copy-start | bytes 4718596
  791.5 18.9 %all-to-all-start.11 = ((bf16[16,16,1024]{2,1,0:T(8,128)(2,1)}), bf16[16,16,1024]{2,1,0:T(8,128)(2,1)}, u32[]{:S(2)}, u32[]{:S(2)}) async-start(bf16[16,16,1024]{2,1,0:T(8,128)(2,1)} %get-tuple-element.43), calls=%async_computation.15 | async-start | bytes 1048576 | tf_op jit(solution)/shard_map/all_to_all | solution.py:92
  810.4 74.7 %all-to-all-start.13 = ((bf16[16,3,64,512]{3,2,1,0:T(8,128)(2,1)}), bf16[16,3,64,512]{3,2,1,0:T(8,128)(2,1)S(1)}, u32[]{:S(2)}, u32[]{:S(2)}) async-start(bf16[16,3,64,512]{3,2,1,0:T(8,128)(2,1)} %copy.109), calls=%async_computation.18 | async-start | bytes 6291456 | tf_op jit(solution)/shard_map/all_to_all | solution.py:92
  885.1 193.7 %all-to-all-start.15 = ((bf16[16,2,64,2048]{3,2,1,0:T(8,128)(2,1)}), bf16[16,2,64,2048]{3,2,1,0:T(8,128)(2,1)}, u32[]{:S(2)}, u32[]{:S(2)}) async-start(bf16[16,2,64,2048]{3,2,1,0:T(8,128)(2,1)} %bitcast.208), calls=%async_computation.20 | async-start | bytes 16777216 | tf_op jit(solution)/shard_map/all_to_all | solution.py:92
  899.5 5.3 copy-start.18
  900.9 172.9 %collective-permute-start.1 = (bf16[2,16,1024]{2,0,1:T(2,128)(2,1)S(1)}, bf16[2,16,1024]{2,0,1:T(2,128)(2,1)S(1)}, u32[]{:S(2)}, u32[]{:S(2)}) collective-permute-start(bf16[2,16,1024]{2,0,1:T(2,128)(2,1)S(1)} %fusion.58), channel_id=1, source_target_pairs={{1,0},{2,1},{3,2},{4,3},{5,4},{6,5},{7,6},{8,7},{9,8},{10,9},{11,1... | collective-permute-start | bytes 196616 | tf_op jit(solution)/shard_map/ppermute | solution.py:15
  1078.8 11.7 %copy-start.1 = (f32[16,1024]{1,0:T(8,128)S(1)}, f32[16,1024]{1,0:T(8,128)}, u32[]{:S(2)}) copy-start(f32[16,1024]{1,0:T(8,128)} %param.11) | copy-start | bytes 196612
Sparse Core Ops, SparseCore 0:
  43.1 20.8 all-gather.4
  418.8 31.3 reduce-scatter.5
  452.9 21.2 all-gather.6
  475.6 21.2 all-gather.8
  521.8 18.6 reduce-scatter.9
  544.5 21.2 all-gather.10
  684.1 19.8 reduce-scatter.11
  706.8 9.8 reduce-scatter.13
  719.5 20.4 reduce-scatter.7

commit v2 on v1

--- a/solution.py
+++ b/solution.py
@@ -98,7 +98,10 @@
 
 
 def grads_to_shards(blocks, positions):
-    arrived = swap(blocks.astype(jnp.bfloat16))
+    return sum_arrived(swap(blocks.astype(jnp.bfloat16)), positions)
+
+
+def sum_arrived(arrived, positions):
     copies = arrived.shape[0] // positions
     parts = arrived.reshape(positions, copies, *arrived.shape[1:]).astype(jnp.float32)
     return jnp.sum(parts, axis=1) if copies > 1 else parts[:, 0]
@@ -161,7 +164,8 @@
     group_cot = flat(both(cot_own))
     full_qkv = weights_to_positions(w_qkv).transpose(1, 0, 2, 3).reshape(3, width, heads_width)
     full_out = weights_to_positions(w_out.transpose(0, 2, 1)).reshape(width, heads_width)
-    full_gu = weights_to_positions(w_gu).transpose(1, 0, 2, 3).reshape(2, width, units)
+    full_gate = weights_to_positions(w_gu[:, 0]).reshape(width, units)
+    full_up = weights_to_positions(w_gu[:, 1]).reshape(width, units)
     full_down = weights_to_positions(w_down.transpose(0, 2, 1)).reshape(width, units)
 
     qkv_pos = matmul(group_norm, full_qkv, "xd,jde->xje").astype(jnp.bfloat16)
@@ -178,9 +182,8 @@
     hidden_in = resid_in + attn_sum
     unit_two, scale_two, normed_two = normalize(hidden_in, ffn_gain)
     group_two = flat(both(normed_two))
-    gate_up = matmul(group_two, full_gu, "xd,jde->jxe")
-    gate_pre = gate_up[0]
-    up_pre = gate_up[1]
+    gate_pre = matmul(group_two, full_gate, "xd,de->xe")
+    up_pre = matmul(group_two, full_up, "xd,de->xe")
     sigmoid_gate = jax.nn.sigmoid(gate_pre)
     silu_gate = gate_pre * sigmoid_gate
     hidden_low = (silu_gate * up_pre).astype(jnp.bfloat16)
@@ -190,16 +193,22 @@
     grad_down = matmul(group_cot, hidden_low, "xd,xe->de")
     grad_hidden = matmul(group_cot, full_down, "xd,de->xe")
     slope = sigmoid_gate * (1.0 + gate_pre * (1.0 - sigmoid_gate))
-    grad_gu = jnp.stack([grad_hidden * up_pre * slope, grad_hidden * silu_gate]).astype(
-        jnp.bfloat16
-    )
-    grad_wgu = matmul(group_two, grad_gu, "xd,jxe->jde")
-    grad_normed_two = own_sum(matmul(grad_gu, full_gu, "jxe,jde->xd").astype(jnp.bfloat16))
+    grad_gate = (grad_hidden * up_pre * slope).astype(jnp.bfloat16)
+    grad_up = (grad_hidden * silu_gate).astype(jnp.bfloat16)
+    grad_wgate = matmul(group_two, grad_gate, "xd,xe->de")
+    grad_wup = matmul(group_two, grad_up, "xd,xe->de")
+    grad_normed_two = own_sum(
+        (
+            matmul(grad_gate, full_gate, "xe,de->xd") + matmul(grad_up, full_up, "xe,de->xd")
+        ).astype(jnp.bfloat16)
+    )
+    moved_down = swap(grad_down.reshape(count, -1, units).astype(jnp.bfloat16))
     back_two, gain_two = norm_back(grad_normed_two, unit_two, scale_two, ffn_gain)
     grad_hidden_in = cot_own.astype(jnp.float32) + back_two
     group_grad = flat(both(grad_hidden_in.astype(jnp.bfloat16)))
     grad_wout = matmul(group_grad, mixed_pos, "xd,xe->de")
     grad_mixed = matmul(group_grad, full_out, "xd,de->xe").astype(jnp.bfloat16)
+    grad_mixed, moved_down = lax.optimization_barrier((grad_mixed, moved_down))
     grad_mixed_low = to_heads(grad_mixed)
     grad_qkv_low = attend_back(qkv_low, grad_mixed_low, log_total, HD)
     grad_qkv = frames_to_rows(
@@ -234,8 +243,10 @@
 
     shard_qkv = grads_to_shards(split_rows(grad_wqkv), positions)
     shard_out = grads_to_shards(grad_wout.reshape(count, -1, heads_width), positions)
-    shard_gu = grads_to_shards(split_rows(grad_wgu), positions)
-    shard_down = grads_to_shards(grad_down.reshape(count, -1, units), positions)
+    shard_gate = grads_to_shards(grad_wgate.reshape(count, -1, units), positions)
+    shard_up = grads_to_shards(grad_wup.reshape(count, -1, units), positions)
+    shard_gu = jnp.stack([shard_gate, shard_up], axis=1)
+    shard_down = sum_arrived(moved_down, positions)
     return (
         result,
         grad_frames,

time: 1100 us -> 1050 us (0.955)
  blocking collectives: 290 us -> 126 us
  waiting for transfers between devices: 500 us -> 583 us
    all_to_all x12 -> x14, waiting for transfers between devices: 213 us -> 392 us  [swap(): return lax.all_to_all(value, 'dp', split_axis=0, concat_axis=0, tiled=True)]
    all_to_all x5, blocking collectives: 290 us -> 126 us  [swap(): return lax.all_to_all(value, 'dp', split_axis=0, concat_axis=0, tiled=True)]
    ppermute x2, waiting for transfers between devices: 168 us -> 43.2 us  [from_behind(): lax.ppermute(value, axis, [(source, source + steps) for source in range(i...]
    all_gather x4, waiting for transfers between devices: 44.9 us -> 70.8 us  [both(): return lax.all_gather(value, 'mp', axis=0, tiled=True)]
    convert_element_type x3 -> x1, other arithmetic: 20 us -> 5.48 us  [sum_arrived(): arrived.reshape(positions, copies, *arrived.shape[1:]).astype(jnp.float32)]
    unnamed x56 -> x57, local copies, waits for them, and re-layouts: 7.01 us -> 19.1 us
    dot_general x12 -> x15, matrix products: 69.5 us -> 79.9 us  [matmul(): return jnp.einsum(spec, left, right, preferred_element_type=jnp.float32)]
    all_to_all x12 -> x14, starting transfers between devices: 62.6 us -> 72.3 us  [swap(): return lax.all_to_all(value, 'dp', split_axis=0, concat_axis=0, tiled=True)]
  transfers between devices with their start and end apart: 23 -> 25, of which waited for: 17 -> 23; matrix products, arithmetic and copies ran while one was open for 17% -> 20% of each run, Pallas kernels for 0% -> 0%
where the time goes in v2:
time: 1050 us; the launch traced here: 1040 us
  waiting for transfers between devices  583 us (56%)
  blocking collectives  126 us (12%)
  local copies, waits for them, and re-layouts  107 us (10%)
  matrix products  89.1 us (8%)
  starting transfers between devices  80.6 us (8%)
  other arithmetic  40.6 us (4%)
  between operations  14.9 us (1%)
    all_to_all x14, waiting for transfers between devices, swap(): return lax.all_to_all(value, 'dp', split_axis=0, concat_axis=0, tiled=True)  392 us
    all_to_all x5, blocking collectives, swap(): return lax.all_to_all(value, 'dp', split_axis=0, concat_axis=0, tiled=True)  126 us
    dot_general x15, matrix products, matmul(): return jnp.einsum(spec, left, right, preferred_element_type=jnp.float32)  79.9 us
    reduce_scatter x4, waiting for transfers between devices, own_sum(): lax.psum_scatter(value.reshape(groups * count, part, width), 'mp', scatte...  72.8 us
    all_to_all x14, starting transfers between devices, swap(): return lax.all_to_all(value, 'dp', split_axis=0, concat_axis=0, tiled=True)  72.3 us
    all_gather x4, waiting for transfers between devices, both(): return lax.all_gather(value, 'mp', axis=0, tiled=True)  70.8 us
    ppermute x2, waiting for transfers between devices, from_behind(): lax.ppermute(value, axis, [(source, source + steps) for source in range(i...  43.2 us
  transfers between devices with their start and end apart: 25, of which 23 were waited for; matrix products, arithmetic and copies ran while one was open for 20% of the time, Pallas kernels for 0%

profile of v2, /device:TPU:15, one launch (start us, length us, event | category | flops | bytes accessed | tf_op | source)
XLA Modules:
  0.0 1040.7 jit_solution(4972483986555116494)
XLA Ops:
  9.4 6.5 all-to-all-start.9
  16.3 3.5 collective-permute-start
  19.9 8.7 collective-permute-done
  30.3 18.3 %all_to_all.95 = bf16[16,16,1024]{2,1,0:T(8,128)(2,1)S(1)} all-to-all(bf16[16,16,1024]{2,1,0:T(8,128)(2,1)S(1)} %fusion.39), channel_id=1, replica_groups=mesh['dp'=16,'mp'=2] {'dp'}, dimensions={0} | all-to-all | bytes 1048576 | tf_op jit(solution)/shard_map/all_to_all | solution.py:92
  48.6 29.6 %all_to_all.96 = bf16[16,64,512]{2,1,0:T(8,128)(2,1)} all-to-all(bf16[16,64,512]{2,1,0:T(8,128)(2,1)S(1)} %bitcast.187), channel_id=1, replica_groups=mesh['dp'=16,'mp'=2] {'dp'}, dimensions={0} | all-to-all | bytes 2097152 | tf_op jit(solution)/shard_map/all_to_all | solution.py:92
  78.1 4.9 all-to-all-start.1
  83.1 6.1 slice_bitcast_fusion.1
  89.2 63.8 %all-to-all-done.1 = bf16[16,3,64,512]{3,2,1,0:T(8,128)(2,1)} async-done(((bf16[16,3,64,512]{3,2,1,0:T(8,128)(2,1)}), bf16[16,3,64,512]{3,2,1,0:T(8,128)(2,1)}, u32[]{:S(2)}, u32[]{:S(2)}) %all-to-all-start.1) | async-done | bytes 3145760 | tf_op jit(solution)/shard_map/all_to_all | solution.py:92
  153.1 4.8 all-to-all-start.5
  159.1 3.9 copy.74
  163.0 19.3 %all-gather.5.cloned.1.call-done = bf16[32,16,1024]{2,1,0:T(8,128)(2,1)} async-done(((bf16[16,16,1024]{2,1,0:T(8,128)(2,1)}), bf16[32,16,1024]{2,1,0:T(8,128)(2,1)}) %all-gather.5.cloned.1.call-update) | async-done | bytes 1048592 | tf_op jit(solution)/shard_map/all_gather | solution.py:128
  182.3 4.0 convolution_convert_fusion.3
  193.5 56.8 %all-to-all-done.5 = bf16[16,64,2048]{2,1,0:T(8,128)(2,1)} async-done(((bf16[16,64,2048]{2,1,0:T(8,128)(2,1)}), bf16[16,64,2048]{2,1,0:T(8,128)(2,1)}, u32[]{:S(2)}, u32[]{:S(2)}) %all-to-all-start.5) | async-done | bytes 4194336 | tf_op jit(solution)/shard_map/all_to_all | solution.py:92
  250.3 40.8 %all_to_all.97 = bf16[16,32,1536]{2,1,0:T(8,128)(2,1)S(1)} all-to-all(bf16[16,32,1536]{2,1,0:T(8,128)(2,1)} %bitcast.171), channel_id=1, replica_groups=mesh['dp'=16,'mp'=2] {'dp'}, dimensions={0} | all-to-all | bytes 3145728 | tf_op jit(solution)/shard_map/all_to_all | solution.py:92
  291.1 5.3 all-to-all-start.6
  298.4 4.6 reshape_reshape.10
  303.0 7.6 slice_reduce_fusion.1
  323.3 65.4 %all-to-all-done.6 = bf16[16,64,2048]{2,1,0:T(8,128)(2,1)} async-done(((bf16[16,64,2048]{2,1,0:T(8,128)(2,1)}), bf16[16,64,2048]{2,1,0:T(8,128)(2,1)}, u32[]{:S(2)}, u32[]{:S(2)}) %all-to-all-start.6) | async-done | bytes 4194336 | tf_op jit(solution)/shard_map/all_to_all | solution.py:92
  388.7 18.2 %all_to_all.98 = bf16[16,32,512]{2,1,0:T(8,128)(2,1)} all-to-all(bf16[16,32,512]{2,1,0:T(8,128)(2,1)S(1)} %copy.83), channel_id=1, replica_groups=mesh['dp'=16,'mp'=2] {'dp'}, dimensions={0} | all-to-all | bytes 1048576 | tf_op jit(solution)/shard_map/all_to_all | solution.py:92
  407.0 5.2 all-to-all-start.7
  417.0 31.5 %reduce-scatter.6.cloned.1.call-done = f32[16,16,1024]{2,1,0:T(8,128)} async-done(((f32[32,16,1024]{2,1,0:T(8,128)}), f32[16,16,1024]{2,1,0:T(8,128)}) %reduce-scatter.6.cloned.1.call-update) | async-done | bytes 1048592 | tf_op jit(solution)/shard_map/reduce_scatter | solution.py:151
  451.7 20.9 %all-gather.7.cloned.1.call-done = bf16[32,16,1024]{2,1,0:T(8,128)(2,1)} async-done(((bf16[16,16,1024]{2,1,0:T(8,128)(2,1)}), bf16[32,16,1024]{2,1,0:T(8,128)(2,1)}) %all-gather.7.cloned.1.call-update) | async-done | bytes 1048592 | tf_op jit(solution)/shard_map/all_gather | solution.py:128
  472.5 6.9 fusion.47
  479.5 6.6 fusion.48
  486.0 9.2 all-gather.9.cloned.1.call-done
  495.2 9.4 all-to-all-done.7
  504.7 10.7 %multiply_convert_fusion = (bf16[512,2048]{1,0:T(8,128)(2,1)}, bf16[512,2048]{1,0:T(8,128)(2,1)}, bf16[512,2048]{1,0:T(8,128)(2,1)S(1)}) fusion(f32[512,2048]{1,0:T(8,128)} %fusion.47, f32[512,2048]{1,0:T(8,128)} %fusion.48, bf16[512,1024]{1,0:T(8,128)(2,1)} %bitcast.212, bf16[1024,2048]{1,0:T(8,128)(2,1)} %bitcast.28), kind=kOutput, calls=%fused_computation.2 | convolution fusion | flops 2163212288 | bytes 19922944 | tf_op jit(solution)/shard_map/xd,de->xe/dot_general | solution.py:132
  515.4 4.4 convolution_convert_fusion.2
  519.9 4.8 all-to-all-start.10
  524.9 5.3 fusion.49
  530.2 5.6 add_convert_fusion
  535.9 20.7 %reduce-scatter.10.cloned.1.call-done = bf16[16,16,1024]{2,1,0:T(8,128)(2,1)} async-done(((bf16[32,16,1024]{2,1,0:T(8,128)(2,1)}), bf16[16,16,1024]{2,1,0:T(8,128)(2,1)}) %reduce-scatter.10.cloned.1.call-update) | async-done | bytes 524304 | tf_op jit(solution)/shard_map/reduce_scatter | solution.py:151
  560.4 21.4 %all-gather.11.cloned.1.call-done = bf16[32,16,1024]{2,1,0:T(8,128)(2,1)} async-done(((bf16[16,16,1024]{2,1,0:T(8,128)(2,1)}), bf16[32,16,1024]{2,1,0:T(8,128)(2,1)}) %all-gather.11.cloned.1.call-update) | async-done | bytes 1048592 | tf_op jit(solution)/shard_map/all_gather | solution.py:128
  587.2 29.9 %all-to-all-done.10 = bf16[16,64,2048]{2,1,0:T(8,128)(2,1)} async-done(((bf16[16,64,2048]{2,1,0:T(8,128)(2,1)}), bf16[16,64,2048]{2,1,0:T(8,128)(2,1)}, u32[]{:S(2)}, u32[]{:S(2)}) %all-to-all-start.10) | async-done | bytes 4194336 | tf_op jit(solution)/shard_map/all_to_all | solution.py:92
  617.1 4.8 all-to-all-start.16
  625.0 21.9 %all-to-all-done.16 = bf16[16,64,512]{2,1,0:T(8,128)(2,1)} async-done(((bf16[16,64,512]{2,1,0:T(8,128)(2,1)}), bf16[16,64,512]{2,1,0:T(8,128)(2,1)}, u32[]{:S(2)}, u32[]{:S(2)}) %all-to-all-start.16) | async-done | bytes 1048608 | tf_op jit(solution)/shard_map/all_to_all | solution.py:92
  646.8 4.8 all-to-all-start.11
  654.0 6.3 convolution_convert_fusion
  660.2 5.1 all-to-all-done.11
  665.3 5.5 all-to-all-start.18
  699.6 63.5 %all-to-all-done.18 = bf16[16,64,2048]{2,1,0:T(8,128)(2,1)} async-done(((bf16[16,64,2048]{2,1,0:T(8,128)(2,1)}), bf16[16,64,2048]{2,1,0:T(8,128)(2,1)}, u32[]{:S(2)}, u32[]{:S(2)}) %all-to-all-start.18) | async-done | bytes 4194336 | tf_op jit(solution)/shard_map/all_to_all | solution.py:92
  763.2 5.1 all-to-all-start.12
  768.2 6.3 convolution_convert_fusion.1
  774.5 29.8 %all-to-all-done.12 = bf16[16,32,1536]{2,1,0:T(8,128)(2,1)S(1)} async-done(((bf16[16,32,1536]{2,1,0:T(8,128)(2,1)}), bf16[16,32,1536]{2,1,0:T(8,128)(2,1)S(1)}, u32[]{:S(2)}, u32[]{:S(2)}) %all-to-all-start.12) | async-done | bytes 1572896 | tf_op jit(solution)/shard_map/all_to_all | solution.py:92
  804.3 4.8 all-to-all-start.17
  810.4 4.6 reshape_reshape.12
  817.8 5.3 bitcast_convert_fusion
  823.2 20.6 %reduce-scatter.12.cloned.1.call-done = bf16[16,16,1024]{2,1,0:T(8,128)(2,1)} async-done(((bf16[32,16,1024]{2,1,0:T(8,128)(2,1)}), bf16[16,16,1024]{2,1,0:T(8,128)(2,1)}) %reduce-scatter.12.cloned.1.call-update) | async-done | bytes 524304 | tf_op jit(solution)/shard_map/reduce_scatter | solution.py:151
  846.2 6.3 convolution_convert_fusion.7
  852.5 4.0 reduce-scatter.14.cloned.1.call-done
  857.8 43.7 %all-to-all-done.17 = bf16[16,64,2048]{2,1,0:T(8,128)(2,1)} async-done(((bf16[16,64,2048]{2,1,0:T(8,128)(2,1)}), bf16[16,64,2048]{2,1,0:T(8,128)(2,1)}, u32[]{:S(2)}, u32[]{:S(2)}) %all-to-all-start.17) | async-done | bytes 4194336 | tf_op jit(solution)/shard_map/all_to_all | solution.py:92
  901.6 4.8 all-to-all-start.14
  910.5 19.4 %all_to_all.99 = bf16[16,16,1024]{2,1,0:T(8,128)(2,1)S(1)} all-to-all(bf16[16,16,1024]{2,1,0:T(8,128)(2,1)} %get-tuple-element.51), channel_id=1, replica_groups=mesh['dp'=16,'mp'=2] {'dp'}, dimensions={0} | all-to-all | bytes 1048576 | tf_op jit(solution)/shard_map/all_to_all | solution.py:92
  929.9 4.8 all-to-all-start.13
  934.7 4.9 convert_bitcast_fusion.1
  939.6 4.6 copy.105
  944.2 3.9 copy.106
  948.3 6.3 all-to-all-start.15
  957.5 10.3 maximum_convert_fusion
  967.8 11.8 %copy.112 = f32[16,2,64,2048]{3,2,1,0:T(8,128)} copy(f32[16,2,64,2048]{3,2,0,1:T(8,128)} %maximum_convert_fusion) | data formatting | bytes 33554432
  979.7 6.7 convert_bitcast_fusion
  986.6 3.8 collective-permute-start.1
  992.1 34.5 %collective-permute-done.1 = bf16[2,16,1024]{2,0,1:T(2,128)(2,1)S(1)} collective-permute-done((bf16[2,16,1024]{2,0,1:T(2,128)(2,1)S(1)}, bf16[2,16,1024]{2,0,1:T(2,128)(2,1)S(1)}, u32[]{:S(2)}, u32[]{:S(2)}) %collective-permute-start.1) | collective-permute-done | bytes 65568 | tf_op jit(solution)/shard_map/ppermute | solution.py:15
  1028.2 5.5 convert_element_type.201
  (149 shorter events, 97.3 us)
Async XLA Ops:
  7.2 150.7 %copy-start = (f32[16,1024]{1,0:T(8,128)S(1)}, f32[16,1024]{1,0:T(8,128)}, u32[]{:S(2)}) copy-start(f32[16,1024]{1,0:T(8,128)} %param.11) | copy-start | bytes 196612
  7.2 8.7 copy-start.20
  7.2 12.6 %copy-start.21 = (s32[16,16]{1,0:T(8,128)S(1)}, s32[16,16]{1,0:T(8,128)}, u32[]{:S(2)}) copy-start(s32[16,16]{1,0:T(8,128)} %param.10) | copy-start | bytes 3076
  9.4 20.1 %all-to-all-start.9 = ((bf16[16,16,1024]{2,1,0:T(8,128)(2,1)}), bf16[16,16,1024]{2,1,0:T(8,128)(2,1)S(1)}, u32[]{:S(2)}, u32[]{:S(2)}) async-start(bf16[16,16,1024]{2,1,0:T(8,128)(2,1)} %bitcast.167), calls=%async_computation.11 | async-start | bytes 1048576 | tf_op jit(solution)/shard_map/all_to_all | solution.py:92
  16.2 32.4 %copy-start.18 = (bf16[16,512,64]{1,2,0:T(8,128)(2,1)S(1)}, bf16[16,512,64]{1,2,0:T(8,128)(2,1)}, u32[]{:S(2)}) copy-start(bf16[16,512,64]{1,2,0:T(8,128)(2,1)} %param.13) | copy-start | bytes 3145732
  16.3 12.3 %collective-permute-start = (bf16[2,16,1024]{2,0,1:T(2,128)(2,1)S(1)}, bf16[2,16,1024]{2,0,1:T(2,128)(2,1)S(1)}, u32[]{:S(2)}, u32[]{:S(2)}) collective-permute-start(bf16[2,16,1024]{2,0,1:T(2,128)(2,1)S(1)} %slice.52), channel_id=1, source_target_pairs={{0,1},{1,2},{2,3},{3,4},{4,5},{5,6},{6,7},{7,8},{8,9},{9,10},{10,1... | collective-permute-start | bytes 196616 | tf_op jit(solution)/shard_map/ppermute | solution.py:15
  29.5 0.8 copy-start.7
  48.6 109.5 %copy-start.2 = (bf16[16,16,1024]{2,1,0:T(8,128)(2,1)}, bf16[16,16,1024]{2,1,0:T(8,128)(2,1)S(1)}, u32[]{:S(2)}) copy-start(bf16[16,16,1024]{2,1,0:T(8,128)(2,1)S(1)} %all_to_all.95) | copy-start | bytes 1572868
  78.1 74.9 %all-to-all-start.1 = ((bf16[16,3,64,512]{3,2,1,0:T(8,128)(2,1)}), bf16[16,3,64,512]{3,2,1,0:T(8,128)(2,1)}, u32[]{:S(2)}, u32[]{:S(2)}) async-start(bf16[16,3,64,512]{3,2,1,0:T(8,128)(2,1)} %param.12), calls=%async_computation.1 | async-start | bytes 6291456 | tf_op jit(solution)/shard_map/all_to_all | solution.py:92
  153.1 97.2 %all-to-all-start.5 = ((bf16[16,64,2048]{2,1,0:T(8,128)(2,1)}), bf16[16,64,2048]{2,1,0:T(8,128)(2,1)}, u32[]{:S(2)}, u32[]{:S(2)}) async-start(bf16[16,64,2048]{2,1,0:T(8,128)(2,1)} %get-tuple-element.48), calls=%async_computation.6 | async-start | bytes 8388608 | tf_op jit(solution)/shard_map/all_to_all | solution.py:92
  157.8 24.5 %all-gather.5.cloned.1.call-start = ((), (), s32[]{:S(2)}) async-start(), calls=%async_computation.24 | async-start | bytes 1572864 | tf_op jit(solution)/shard_map/all_gather | solution.py:128
  291.1 97.6 %all-to-all-start.6 = ((bf16[16,64,2048]{2,1,0:T(8,128)(2,1)}), bf16[16,64,2048]{2,1,0:T(8,128)(2,1)}, u32[]{:S(2)}, u32[]{:S(2)}) async-start(bf16[16,64,2048]{2,1,0:T(8,128)(2,1)} %get-tuple-element.49), calls=%async_computation.7 | async-start | bytes 8388608 | tf_op jit(solution)/shard_map/all_to_all | solution.py:92
  310.7 4.4 copy-start.13
  312.4 7.3 copy-start.6
  407.0 7.2 copy-start.10
  407.0 97.7 %all-to-all-start.7 = ((bf16[16,64,2048]{2,1,0:T(8,128)(2,1)}), bf16[16,64,2048]{2,1,0:T(8,128)(2,1)}, u32[]{:S(2)}, u32[]{:S(2)}) async-start(bf16[16,64,2048]{2,1,0:T(8,128)(2,1)} %bitcast.177), calls=%async_computation.8 | async-start | bytes 8388608 | tf_op jit(solution)/shard_map/all_to_all | solution.py:92
  412.2 36.3 %reduce-scatter.6.cloned.1.call-start = ((), (), s32[]{:S(2)}) async-start(), calls=%async_computation.25 | async-start | bytes 3145728 | tf_op jit(solution)/shard_map/reduce_scatter | solution.py:151
  413.3 0.8 copy-start.14
  416.2 56.3 %all-gather.7.cloned.1.call-start = ((), (), s32[]{:S(2)}) async-start(), calls=%async_computation.26 | async-start | bytes 1572864 | tf_op jit(solution)/shard_map/all_gather | solution.py:128
  451.1 44.2 %all-gather.9.cloned.1.call-start = ((), (), s32[]{:S(2)}) async-start(), calls=%async_computation.28 | async-start | bytes 1572864 | tf_op jit(solution)/shard_map/all_gather | solution.py:128
  472.5 6.9 copy-start.19
  504.7 10.7 %copy-start.23 = (bf16[32,16,1024]{2,1,0:T(8,128)(2,1)S(1)}, bf16[32,16,1024]{2,1,0:T(8,128)(2,1)}, u32[]{:S(2)}) copy-start(bf16[32,16,1024]{2,1,0:T(8,128)(2,1)} %all-gather.9.cloned.1.call-done) | copy-start | bytes 3145732
  515.4 4.4 copy-start.25
  519.9 97.2 %all-to-all-start.10 = ((bf16[16,64,2048]{2,1,0:T(8,128)(2,1)}), bf16[16,64,2048]{2,1,0:T(8,128)(2,1)}, u32[]{:S(2)}, u32[]{:S(2)}) async-start(bf16[16,64,2048]{2,1,0:T(8,128)(2,1)} %bitcast.178), calls=%async_computation.13 | async-start | bytes 8388608 | tf_op jit(solution)/shard_map/all_to_all | solution.py:92
  524.6 32.0 %reduce-scatter.10.cloned.1.call-start = ((), (), s32[]{:S(2)}) async-start(), calls=%async_computation.29 | async-start | bytes 1572864 | tf_op jit(solution)/shard_map/reduce_scatter | solution.py:151
  524.8 5.3 copy-start.24
  535.8 46.0 %all-gather.11.cloned.1.call-start = ((), (), s32[]{:S(2)}) async-start(), calls=%async_computation.30 | async-start | bytes 1572864 | tf_op jit(solution)/shard_map/all_gather | solution.py:128
  617.1 29.7 %all-to-all-start.16 = ((bf16[16,64,512]{2,1,0:T(8,128)(2,1)}), bf16[16,64,512]{2,1,0:T(8,128)(2,1)}, u32[]{:S(2)}, u32[]{:S(2)}) async-start(bf16[16,64,512]{2,1,0:T(8,128)(2,1)} %convolution_convert_fusion.6), calls=%async_computation.21 | async-start | bytes 2097152 | tf_op jit(solution)/shard_map/all_to_all | solution.py:92
  646.8 18.5 %all-to-all-start.11 = ((bf16[16,32,512]{2,1,0:T(8,128)(2,1)}), bf16[16,32,512]{2,1,0:T(8,128)(2,1)}, u32[]{:S(2)}, u32[]{:S(2)}) async-start(bf16[16,32,512]{2,1,0:T(8,128)(2,1)} %bitcast.185), calls=%async_computation.14 | async-start | bytes 1048576 | tf_op jit(solution)/shard_map/all_to_all | solution.py:92
  665.3 97.8 %all-to-all-start.18 = ((bf16[16,64,2048]{2,1,0:T(8,128)(2,1)}), bf16[16,64,2048]{2,1,0:T(8,128)(2,1)}, u32[]{:S(2)}, u32[]{:S(2)}) async-start(bf16[16,64,2048]{2,1,0:T(8,128)(2,1)} %convolution_convert_fusion), calls=%async_computation.23 | async-start | bytes 8388608 | tf_op jit(solution)/shard_map/all_to_all | solution.py:92
  682.0 1.6 copy-start.12
  682.7 1.0 copy-start.4
  684.3 3.8 copy-start.5
  684.3 3.8 copy-start.11
  688.7 1.7 copy-start.16
  688.7 1.7 copy-start.17
  763.2 41.2 %all-to-all-start.12 = ((bf16[16,32,1536]{2,1,0:T(8,128)(2,1)}), bf16[16,32,1536]{2,1,0:T(8,128)(2,1)S(1)}, u32[]{:S(2)}, u32[]{:S(2)}) async-start(bf16[16,32,1536]{2,1,0:T(8,128)(2,1)} %copy.98), calls=%async_computation.15 | async-start | bytes 3145728 | tf_op jit(solution)/shard_map/all_to_all | solution.py:92
  804.3 97.2 %all-to-all-start.17 = ((bf16[16,64,2048]{2,1,0:T(8,128)(2,1)}), bf16[16,64,2048]{2,1,0:T(8,128)(2,1)}, u32[]{:S(2)}, u32[]{:S(2)}) async-start(bf16[16,64,2048]{2,1,0:T(8,128)(2,1)} %convolution_convert_fusion.1), calls=%async_computation.22 | async-start | bytes 8388608 | tf_op jit(solution)/shard_map/all_to_all | solution.py:92
  809.1 34.7 %reduce-scatter.12.cloned.1.call-start = ((), (), s32[]{:S(2)}) async-start(), calls=%async_computation.31 | async-start | bytes 1572864 | tf_op jit(solution)/shard_map/reduce_scatter | solution.py:151
  817.8 26.1 %copy-start.3 = (bf16[16,16,1024]{2,1,0:T(8,128)(2,1)S(1)}, bf16[16,16,1024]{2,1,0:T(8,128)(2,1)}, u32[]{:S(2)}) copy-start(bf16[16,16,1024]{2,1,0:T(8,128)(2,1)} %copy-done.2) | copy-start | bytes 1572868
  823.1 33.4 %reduce-scatter.14.cloned.1.call-start = ((), (), s32[]{:S(2)}) async-start(), calls=%async_computation.32 | async-start | bytes 49152 | tf_op jit(solution)/shard_map/reduce_scatter | solution.py:234
  846.1 60.3 %copy-start.8 = (bf16[16,16,1024]{2,1,0:T(8,128)(2,1)S(1)}, bf16[16,16,1024]{2,1,0:T(8,128)(2,1)}, u32[]{:S(2)}) copy-start(bf16[16,16,1024]{2,1,0:T(8,128)(2,1)} %copy-done.7) | copy-start | bytes 1572868
  846.1 60.3 %copy-start.9 = (bf16[16,16,1024]{2,1,0:T(8,128)(2,1)S(1)}, bf16[16,16,1024]{2,1,0:T(8,128)(2,1)}, u32[]{:S(2)}) copy-start(bf16[16,16,1024]{2,1,0:T(8,128)(2,1)} %reduce-scatter.10.cloned.1.call-done) | copy-start | bytes 1572868
  846.1 60.3 %copy-start.15 = (bf16[16,16,1024]{2,1,0:T(8,128)(2,1)S(1)}, bf16[16,16,1024]{2,1,0:T(8,128)(2,1)}, u32[]{:S(2)}) copy-start(bf16[16,16,1024]{2,1,0:T(8,128)(2,1)} %reduce-scatter.12.cloned.1.call-done) | copy-start | bytes 1572868
  846.1 60.2 %reduce-scatter.8.cloned.1.call-start = ((), (), s32[]{:S(2)}) async-start(), calls=%async_computation.27 | async-start | bytes 1572864 | tf_op jit(solution)/shard_map/reduce_scatter | solution.py:151
  901.6 8.9 all-to-all-start.14
  909.0 25.7 %copy-start.22 = (bf16[32,16,1024]{2,1,0:T(8,128)(2,1)S(1)}, bf16[32,16,1024]{2,1,0:T(8,128)(2,1)}, u32[]{:S(2)}) copy-start(bf16[32,16,1024]{2,1,0:T(8,128)(2,1)} %all-gather.5.cloned.1.call-done) | copy-start | bytes 3145732
  929.9 18.4 %all-to-all-start.13 = ((bf16[16,16,1024]{2,1,0:T(8,128)(2,1)}), bf16[16,16,1024]{2,1,0:T(8,128)(2,1)S(1)}, u32[]{:S(2)}, u32[]{:S(2)}) async-start(bf16[16,16,1024]{2,1,0:T(8,128)(2,1)} %get-tuple-element.50), calls=%async_computation.17 | async-start | bytes 1048576 | tf_op jit(solution)/shard_map/all_to_all | solution.py:92
  948.3 79.9 %all-to-all-start.15 = ((bf16[16,3,64,512]{3,2,1,0:T(8,128)(2,1)}), bf16[16,3,64,512]{3,2,1,0:T(8,128)(2,1)}, u32[]{:S(2)}, u32[]{:S(2)}) async-start(bf16[16,3,64,512]{3,2,1,0:T(8,128)(2,1)} %copy.106), calls=%async_computation.20 | async-start | bytes 6291456 | tf_op jit(solution)/shard_map/all_to_all | solution.py:92
  986.6 40.0 %collective-permute-start.1 = (bf16[2,16,1024]{2,0,1:T(2,128)(2,1)S(1)}, bf16[2,16,1024]{2,0,1:T(2,128)(2,1)S(1)}, u32[]{:S(2)}, u32[]{:S(2)}) collective-permute-start(bf16[2,16,1024]{2,0,1:T(2,128)(2,1)S(1)} %fusion.43), channel_id=1, source_target_pairs={{1,0},{2,1},{3,2},{4,3},{5,4},{6,5},{7,6},{8,7},{9,8},{10,9},{11,1... | collective-permute-start | bytes 196616 | tf_op jit(solution)/shard_map/ppermute | solution.py:15
  1028.2 5.5 copy-start.1
Sparse Core Ops, SparseCore 0:
  160.8 21.4 all-gather.4
  416.3 32.1 reduce-scatter.5
  451.2 21.2 all-gather.6
  473.9 21.2 all-gather.8
  535.9 20.5 reduce-scatter.9
  560.5 21.2 all-gather.10
  823.2 20.5 reduce-scatter.11
  846.6 9.8 reduce-scatter.13
  859.3 20.4 reduce-scatter.7
